TPU v7x, 256 devices: a whole 4x4x8 slice. The times are simulated.
256 devices in a mesh: cache: 8 (over z_hi, core), expert: 32 (over x, z_lo, y).
Axes of the slice: x: 4, y: 4, z: 8 (z_hi: 4, z_lo: 2; z = z_hi * 2 + z_lo), core: 2. Of those that a mesh axis runs over, the one named last changes fastest.
Arguments:
- queries: bfloat16 [2, 128, 2048], P(None, 'expert'), may hold values from -16 to 16
- k_cache: bfloat16 [128, 8192, 256], P('expert', 'cache'), may hold values from -6 to 6
- v_cache: bfloat16 [128, 8192, 256], P('expert', 'cache'), may hold values from -6 to 6
- lengths: int32 [128], P('expert'), may hold values from 1 to 8190
- w_out: bfloat16 [2048, 2880], P('cache'), may hold values from -0.125 to 0.125
- norm_gain: float32 [2880], replicated, may hold values from 0.25 to 1.75
- w_gate: bfloat16 [32, 2880, 1440], P('cache', 'expert'), may hold values from -0.109375 to 0.109375
- w_up: bfloat16 [32, 2880, 1440], P('cache', 'expert'), may hold values from -0.109375 to 0.109375
- w_down: bfloat16 [32, 1440, 2880], P('cache', None, 'expert'), may hold values from -0.15625 to 0.15625
- expert_ids: int32 [2, 128, 4], P(None, 'expert'), may hold values from 0 to 31, all different within a row; in each aligned block of 4 rows (0 to 3, 4 to 7, ..., all dimensions but the last counted through in order) at most 2 rows name the same one
- gate_weights: float32 [2, 128, 4], P(None, 'expert'), may hold values from 0.1 to 1
Outputs:
- mixed: bfloat16 [2, 128, 2880], P(None, 'expert')
- gate_owner: bfloat16 [32, 2880, 1440], P('expert', None, 'cache')
- up_owner: bfloat16 [32, 2880, 1440], P('expert', None, 'cache')
- down_owner: bfloat16 [32, 1440, 2880], P('expert', 'cache')
Inputs may be any that keep to these rules, and one draw needn't show every extreme that they name: `expert_ids`: in each step the 4 rows of one index of expert name one expert at most 2 times; a row names 4 different experts.
All inputs are finite; a program needn't handle non-finite values.
Results may differ from a plain program's by a relative error of at most 0.015.
Values may be sent and summed in bfloat16 or wider, within the bound.
No kernel may reach another device: no remote copies, remote signals or barrier semaphores. Data moves between devices by JAX's collectives and lax.ppermute only.
A program may use at most 64 MiB of HBM per device.

v0:
```python
import math

import jax
import jax.numpy as jnp
from jax import lax
from jax.sharding import PartitionSpec as P

D = 2880
QH = 32
KVH = 4
HD = 64
TOP = 4


def side_by_side(arrays, axis, split_dim, concat_dim, along):
    widths = [a.shape[along] for a in arrays]
    both = jnp.concatenate(arrays, axis=along)
    filled = lax.all_to_all(both, axis, split_axis=split_dim, concat_axis=concat_dim, tiled=True)
    return tuple(jnp.split(filled, [sum(widths[:k]) for k in range(1, len(widths))], axis=along))


def sent_to_all(shard, axis):
    length = lax.axis_size(axis)
    return lax.all_to_all(
        jnp.broadcast_to(shard[None], (length, *shard.shape)), axis, 0, 0, tiled=True
    )


def over_copies(shard, axis):
    everything = sent_to_all(shard, axis)
    return jnp.sum(everything, axis=0)


def split_up(shard, dim, length):
    before, after = (shard.shape[:dim], shard.shape[dim + 1 :])
    return jnp.moveaxis(shard.reshape(*before, length, -1, *after), dim, 0)


def sum_at_owner(shard, axis, dim):
    length = lax.axis_size(axis)
    tiles = lax.all_to_all(split_up(shard, dim, length), axis, 0, 0, tiled=True)
    return jnp.sum(tiles, axis=0)


def laid_out(tiles, dim):
    tiles = jnp.moveaxis(tiles, 0, dim)
    dims = tiles.shape
    return tiles.reshape(*dims[:dim], dims[dim] * dims[dim + 1], *dims[dim + 2 :])


def gathered_copies(shard, axis, dim):
    return laid_out(sent_to_all(shard, axis), dim)


def shards(
    queries,
    k_cache,
    v_cache,
    lengths,
    w_out,
    norm_gain,
    w_gate,
    w_up,
    w_down,
    expert_ids,
    gate_weights,
):
    gate_owner, up_owner = (
        lax.all_to_all(
            lax.all_to_all(w_gate, "cache", split_axis=2, concat_axis=0, tiled=True),
            "expert",
            split_axis=0,
            concat_axis=1,
            tiled=True,
        ),
        lax.all_to_all(
            lax.all_to_all(w_up, "cache", split_axis=2, concat_axis=0, tiled=True),
            "expert",
            split_axis=0,
            concat_axis=1,
            tiled=True,
        ),
    )
    down_owner = lax.all_to_all(
        lax.all_to_all(w_down, "cache", split_axis=1, concat_axis=0, tiled=True),
        "expert",
        split_axis=0,
        concat_axis=2,
        tiled=True,
    )
    cache_count = lax.axis_size("cache")
    cache_place = lax.axis_index("cache")
    step_count = queries.shape[0]
    row_count = k_cache.shape[0]
    positions = k_cache.shape[1]
    group_size = QH // KVH
    query_heads = queries.reshape(step_count, row_count, KVH, group_size, HD)
    key_heads = k_cache.reshape(row_count, positions, KVH, HD)
    value_heads = v_cache.reshape(row_count, positions, KVH, HD)
    scores = jnp.einsum(
        "srhgd,rphd->srhgp", query_heads, key_heads, preferred_element_type=jnp.float32
    ) * (1.0 / math.sqrt(HD))
    position = cache_place * positions + jnp.arange(positions, dtype=jnp.int32)
    limit = lengths[None, :] + jnp.arange(step_count, dtype=jnp.int32)[:, None] + 1
    visible = (position[None, None, :] < limit[:, :, None])[:, :, None, None, :]
    highest = jnp.max(jnp.where(visible, scores, -1e30), axis=-1)
    weights = jnp.where(visible, jnp.exp(scores - highest[..., None]), 0.0)
    mass = jnp.sum(weights, axis=-1).reshape(step_count, row_count, QH)
    accum = jnp.einsum(
        "srhgp,rphd->srhgd",
        weights.astype(jnp.bfloat16),
        value_heads,
        preferred_element_type=jnp.float32,
    )
    accum = accum.reshape(step_count, row_count, QH * HD)
    highest = highest.reshape(step_count, row_count, QH)
    own_width = w_out.shape[0]
    part_high, part_mass, part_accum = (
        *side_by_side((highest[None], mass[None]), "cache", 3, 0, 1),
        lax.all_to_all(accum[None], "cache", split_axis=3, concat_axis=0, tiled=True),
    )
    shared = jnp.max(part_high, axis=0)
    factor = jnp.exp(part_high - shared[None])
    summed = jnp.sum(part_mass * factor, axis=0)
    weighted = jnp.sum(part_accum * jnp.repeat(factor, HD, axis=-1), axis=0)
    own_out = weighted / jnp.repeat(summed, HD, axis=-1)
    own_rows = own_out.astype(jnp.bfloat16).reshape(step_count * row_count, own_width)
    projected = jnp.dot(own_rows, w_out, preferred_element_type=jnp.float32)
    attention = over_copies(projected, "cache")
    scale = lax.rsqrt(jnp.mean(attention * attention, axis=-1, keepdims=True) + 1e-05)
    normed = (attention * scale * norm_gain).astype(jnp.bfloat16).reshape(step_count, row_count, D)
    experts_total = w_gate.shape[0] * cache_count
    capacity = max(2, (row_count * TOP + experts_total - 1) // experts_total)
    expert_range = jnp.arange(experts_total, dtype=jnp.int32)
    onehot = (expert_ids[..., None] == expert_range).astype(jnp.float32)
    chosen = jnp.sum(onehot, axis=2)
    gate_map = jnp.sum(onehot * gate_weights[..., None], axis=2)
    earlier = jnp.tril(jnp.ones((row_count, row_count), jnp.float32), -1)
    ranks = jnp.einsum("rq,sqe->sre", earlier, chosen, precision=lax.Precision.HIGHEST)
    slot_table = (ranks[..., None] == jnp.arange(capacity, dtype=jnp.float32)).astype(
        jnp.float32
    ) * chosen[..., None]
    outgoing = jnp.einsum(
        "srec,srd->escd",
        slot_table.astype(jnp.bfloat16),
        normed,
        preferred_element_type=jnp.float32,
    )
    outgoing = outgoing.astype(jnp.bfloat16).reshape(experts_total, step_count * capacity, D)
    slots = lax.all_to_all(outgoing, "expert", split_axis=0, concat_axis=0, tiled=True)
    source_count = slots.shape[0]
    item_count = slots.shape[1]
    slot_rows = slots.reshape(source_count * item_count, D)
    gate_value = jnp.dot(slot_rows, gate_owner[0], preferred_element_type=jnp.float32)
    up_value = jnp.dot(slot_rows, up_owner[0], preferred_element_type=jnp.float32)
    hidden = (jax.nn.silu(gate_value) * up_value).astype(jnp.bfloat16)
    partial_out = jnp.dot(hidden, down_owner[0], preferred_element_type=jnp.float32).reshape(
        source_count, item_count, D
    )
    expert_out = sum_at_owner(partial_out, "cache", 2).astype(jnp.bfloat16)
    returned = lax.all_to_all(expert_out, "expert", split_axis=0, concat_axis=0, tiled=True)
    back_width = returned.shape[-1]
    returned = returned.reshape(experts_total, step_count, capacity, back_width)
    combined = jnp.einsum(
        "srec,escd->srd",
        slot_table * gate_map[..., None],
        returned.astype(jnp.float32),
        precision=lax.Precision.HIGHEST,
    )
    attention_rows = attention.reshape(step_count, row_count, D)
    column_block = lax.dynamic_slice_in_dim(attention_rows, cache_place * back_width, back_width, 2)
    mixed = gathered_copies((column_block + combined).astype(jnp.bfloat16), "cache", 2)
    return (mixed, gate_owner, up_owner, down_owner)


def solution(mesh):
    return jax.shard_map(
        shards,
        mesh=mesh,
        in_specs=(
            P(None, "expert", None),
            P("expert", "cache", None),
            P("expert", "cache", None),
            P("expert"),
            P("cache", None),
            P(),
            P("cache", "expert", None),
            P("cache", "expert", None),
            P("cache", None, "expert"),
            P(None, "expert", None),
            P(None, "expert", None),
        ),
        out_specs=(
            P(None, "expert", None),
            P("expert", None, "cache"),
            P("expert", None, "cache"),
            P("expert", "cache", None),
        ),
        check_vma=False,
    )
```

profile of v0, /device:TPU:1, one launch (start us, length us, event | category | flops | bytes accessed | tf_op | source)
XLA Modules:
  0.0 401.4 jit_solution(7815356044981653867)
XLA Ops:
  9.1 10.0 %all-to-all-start.1 = ((f32[1,4,4,32]{2,1,0,3:T(4,128)}), f32[1,4,4,32]{2,1,0,3:T(4,128)S(1)}, u32[]{:S(2)}, u32[]{:S(2)}) async-start(f32[1,4,4,32]{2,1,0,3:T(4,128)} %copy.152), calls=%async_computation.1 | async-start | bytes 131072 | tf_op jit(solution)/shard_map/all_to_all | solution.py:18
  27.7 5.4 %reshape.131 = f32[8,1,2048]{2,1,0:T(1,128)} reshape(f32[2048,1,2,4]{3,2,1,0:T(2,128)} %bitcast.100) | data formatting | bytes 131072
  33.1 7.2 %all-to-all-start = ((f32[8,1,2048]{2,1,0:T(1,128)}), f32[8,1,2048]{2,1,0:T(1,128)S(1)}, u32[]{:S(2)}, u32[]{:S(2)}) async-start(f32[8,1,2048]{2,1,0:T(1,128)} %reshape.131), calls=%async_computation | async-start | bytes 131072 | tf_op jit(solution)/shard_map/all_to_all | solution.py:120
  41.2 6.4 %all-to-all-done = f32[8,1,2048]{2,1,0:T(1,128)S(1)} async-done(((f32[8,1,2048]{2,1,0:T(1,128)}), f32[8,1,2048]{2,1,0:T(1,128)S(1)}, u32[]{:S(2)}, u32[]{:S(2)}) %all-to-all-start) | async-done | bytes 65568 | tf_op jit(solution)/shard_map/all_to_all | solution.py:120
  48.9 4.6 %reshape.132 = f32[2048,1,2,4]{3,2,1,0:T(2,128)} reshape(f32[8,2048]{1,0:T(8,128)S(1)} %reduce) | data formatting | bytes 131072
  58.5 4.5 %all-to-all-start.2 = ((f32[8,8,2880]{2,1,0:T(8,128)}), f32[8,8,2880]{2,1,0:T(8,128)S(1)}, u32[]{:S(2)}, u32[]{:S(2)}) async-start(f32[8,8,2880]{2,1,0:T(8,128)} %broadcast_in_dim.31), calls=%async_computation.2 | async-start | bytes 1507328 | tf_op jit(solution)/shard_map/all_to_all | solution.py:24
  65.5 15.9 %all-to-all-done.2 = f32[8,8,2880]{2,1,0:T(8,128)S(1)} async-done(((f32[8,8,2880]{2,1,0:T(8,128)}), f32[8,8,2880]{2,1,0:T(8,128)S(1)}, u32[]{:S(2)}, u32[]{:S(2)}) %all-to-all-start.2) | async-done | bytes 737312 | tf_op jit(solution)/shard_map/all_to_all | solution.py:24
  82.3 8.1 %all-to-all-start.4 = ((bf16[4,90,1440]{1,0,2:T(4,128)(2,1)}), bf16[4,90,1440]{1,0,2:T(4,128)(2,1)S(1)}, u32[]{:S(2)}, u32[]{:S(2)}) async-start(bf16[4,90,1440]{1,0,2:T(4,128)(2,1)} %copy.157), calls=%async_computation.4 | async-start | bytes 2949120 | tf_op jit(solution)/shard_map/all_to_all | solution.py:70
  94.3 27.8 %all-to-all-done.4 = bf16[4,90,1440]{1,0,2:T(4,128)(2,1)S(1)} async-done(((bf16[4,90,1440]{1,0,2:T(4,128)(2,1)}), bf16[4,90,1440]{1,0,2:T(4,128)(2,1)S(1)}, u32[]{:S(2)}, u32[]{:S(2)}) %all-to-all-start.4) | async-done | bytes 1036832 | tf_op jit(solution)/shard_map/all_to_all | solution.py:70
  123.2 10.2 %all-to-all-start.6 = ((bf16[4,90,1440]{1,0,2:T(4,128)(2,1)}), bf16[4,90,1440]{1,0,2:T(4,128)(2,1)S(1)}, u32[]{:S(2)}, u32[]{:S(2)}) async-start(bf16[4,90,1440]{1,0,2:T(4,128)(2,1)} %copy.160), calls=%async_computation.6 | async-start | bytes 2949120 | tf_op jit(solution)/shard_map/all_to_all | solution.py:77
  137.3 27.3 %all-to-all-done.6 = bf16[4,90,1440]{1,0,2:T(4,128)(2,1)S(1)} async-done(((bf16[4,90,1440]{1,0,2:T(4,128)(2,1)}), bf16[4,90,1440]{1,0,2:T(4,128)(2,1)S(1)}, u32[]{:S(2)}, u32[]{:S(2)}) %all-to-all-start.6) | async-done | bytes 1036832 | tf_op jit(solution)/shard_map/all_to_all | solution.py:77
  165.7 10.7 %all-to-all-start.8 = ((bf16[4,1440,90]{2,0,1:T(4,128)(2,1)}), bf16[4,1440,90]{2,0,1:T(4,128)(2,1)S(1)}, u32[]{:S(2)}, u32[]{:S(2)}) async-start(bf16[4,1440,90]{2,0,1:T(4,128)(2,1)} %copy.164), calls=%async_computation.8 | async-start | bytes 2949120 | tf_op jit(solution)/shard_map/all_to_all | solution.py:85
  179.9 28.3 %all-to-all-done.8 = bf16[4,1440,90]{2,0,1:T(4,128)(2,1)S(1)} async-done(((bf16[4,1440,90]{2,0,1:T(4,128)(2,1)}), bf16[4,1440,90]{2,0,1:T(4,128)(2,1)S(1)}, u32[]{:S(2)}, u32[]{:S(2)}) %all-to-all-start.8) | async-done | bytes 1036832 | tf_op jit(solution)/shard_map/all_to_all | solution.py:85
  208.2 13.6 %all-to-all-start.3 = ((bf16[32,4,2880]{2,1,0:T(4,128)(2,1)}), bf16[32,4,2880]{2,1,0:T(4,128)(2,1)}, u32[]{:S(2)}, u32[]{:S(2)}) async-start(bf16[32,4,2880]{2,1,0:T(4,128)(2,1)} %copy.156), calls=%async_computation.3 | async-start | bytes 1507328 | tf_op jit(solution)/shard_map/all_to_all | solution.py:150
  224.5 9.5 %all-to-all-done.3 = bf16[32,4,2880]{2,1,0:T(4,128)(2,1)} async-done(((bf16[32,4,2880]{2,1,0:T(4,128)(2,1)}), bf16[32,4,2880]{2,1,0:T(4,128)(2,1)}, u32[]{:S(2)}, u32[]{:S(2)}) %all-to-all-start.3) | async-done | bytes 737312 | tf_op jit(solution)/shard_map/all_to_all | solution.py:150
  241.0 16.7 %all-to-all-done.5 = bf16[32,90,180]{1,2,0:T(8,128)(2,1)S(1)} async-done(((bf16[32,90,180]{1,2,0:T(8,128)(2,1)}), bf16[32,90,180]{1,2,0:T(8,128)(2,1)S(1)}, u32[]{:S(2)}, u32[]{:S(2)}) %all-to-all-start.5) | async-done | bytes 1036832 | tf_op jit(solution)/shard_map/all_to_all | solution.py:69
  258.9 4.7 %all-to-all-start.7 = ((bf16[32,90,180]{1,2,0:T(8,128)(2,1)}), bf16[32,90,180]{1,2,0:T(8,128)(2,1)}, u32[]{:S(2)}, u32[]{:S(2)}) async-start(bf16[32,90,180]{1,2,0:T(8,128)(2,1)} %bitcast.102), calls=%async_computation.7 | async-start | bytes 3014656 | tf_op jit(solution)/shard_map/all_to_all | solution.py:76
  266.4 16.1 %all-to-all-done.7 = bf16[32,90,180]{1,2,0:T(8,128)(2,1)} async-done(((bf16[32,90,180]{1,2,0:T(8,128)(2,1)}), bf16[32,90,180]{1,2,0:T(8,128)(2,1)}, u32[]{:S(2)}, u32[]{:S(2)}) %all-to-all-start.7) | async-done | bytes 1036832 | tf_op jit(solution)/shard_map/all_to_all | solution.py:76
  282.5 5.3 %all-to-all-start.9 = ((bf16[32,180,90]{2,1,0:T(8,128)(2,1)}), bf16[32,180,90]{2,1,0:T(8,128)(2,1)}, u32[]{:S(2)}, u32[]{:S(2)}) async-start(bf16[32,180,90]{2,1,0:T(8,128)(2,1)} %bitcast.32), calls=%async_computation.9 | async-start | bytes 3014656 | tf_op jit(solution)/shard_map/all_to_all | solution.py:84
  291.7 4.4 %squeeze.9 = bf16[2880,180]{0,1:T(8,128)(2,1)} reshape(bf16[32,90,180]{1,0,2:T(8,128)(2,1)S(1)} %copy.159) | data formatting | bytes 2073600 | tf_op jit(solution)/shard_map/squeeze | solution.py:154
  318.7 40.3 %all_to_all.157 = f32[8,32,4,360]{3,1,2,0:T(8,128)} all-to-all(f32[8,32,4,360]{3,1,2,0:T(8,128)S(1)} %copy.169), channel_id=1, replica_groups=mesh['cache'=8,'expert'=32] {'cache'}, dimensions={0} | all-to-all | bytes 2949120 | tf_op jit(solution)/shard_map/all_to_all | solution.py:41
  361.2 12.7 %all-to-all-start.11 = ((bf16[32,4,360]{2,1,0:T(4,128)(2,1)}), bf16[32,4,360]{2,1,0:T(4,128)(2,1)S(1)}, u32[]{:S(2)}, u32[]{:S(2)}) async-start(bf16[32,4,360]{2,1,0:T(4,128)(2,1)} %copy.170), calls=%async_computation.11 | async-start | bytes 196608 | tf_op jit(solution)/shard_map/all_to_all | solution.py:161
  373.9 7.5 %all-to-all-done.11 = bf16[32,4,360]{2,1,0:T(4,128)(2,1)S(1)} async-done(((bf16[32,4,360]{2,1,0:T(4,128)(2,1)}), bf16[32,4,360]{2,1,0:T(4,128)(2,1)S(1)}, u32[]{:S(2)}, u32[]{:S(2)}) %all-to-all-start.11) | async-done | bytes 92192 | tf_op jit(solution)/shard_map/all_to_all | solution.py:161
  382.3 5.3 %all-to-all-start.12 = ((bf16[8,2,4,360]{3,2,1,0:T(4,128)(2,1)}), bf16[8,2,4,360]{3,2,1,0:T(4,128)(2,1)S(1)}, u32[]{:S(2)}, u32[]{:S(2)}) async-start(bf16[8,2,4,360]{3,2,1,0:T(4,128)(2,1)} %broadcast_in_dim.32), calls=%async_computation.12 | async-start | bytes 98304 | tf_op jit(solution)/shard_map/all_to_all | solution.py:24
  (102 shorter events, 98.0 us)
Async XLA Ops:
  0.6 56.4 %copy-start = (bf16[256,2880]{0,1:T(8,128)(2,1)S(1)}, bf16[256,2880]{0,1:T(8,128)(2,1)}, u32[]{:S(2)}) copy-start(bf16[256,2880]{0,1:T(8,128)(2,1)} %param.15) | copy-start | bytes 4423684
  1.5 4.0 copy-start.11
  9.1 24.0 %all-to-all-start.1 = ((f32[1,4,4,32]{2,1,0,3:T(4,128)}), f32[1,4,4,32]{2,1,0,3:T(4,128)S(1)}, u32[]{:S(2)}, u32[]{:S(2)}) async-start(f32[1,4,4,32]{2,1,0,3:T(4,128)} %copy.152), calls=%async_computation.1 | async-start | bytes 131072 | tf_op jit(solution)/shard_map/all_to_all | solution.py:18
  33.1 14.5 %all-to-all-start = ((f32[8,1,2048]{2,1,0:T(1,128)}), f32[8,1,2048]{2,1,0:T(1,128)S(1)}, u32[]{:S(2)}, u32[]{:S(2)}) async-start(f32[8,1,2048]{2,1,0:T(1,128)} %reshape.131), calls=%async_computation | async-start | bytes 131072 | tf_op jit(solution)/shard_map/all_to_all | solution.py:120
  53.5 1.6 copy-start.2
  57.6 5.5 %copy-start.10 = (bf16[4,90,1440]{2,0,1:T(4,128)(2,1)S(1)}, bf16[4,90,1440]{2,0,1:T(4,128)(2,1)}, u32[]{:S(2)}) copy-start(bf16[4,90,1440]{2,0,1:T(4,128)(2,1)} %param.17) | copy-start | bytes 3110404
  58.5 22.9 %all-to-all-start.2 = ((f32[8,8,2880]{2,1,0:T(8,128)}), f32[8,8,2880]{2,1,0:T(8,128)S(1)}, u32[]{:S(2)}, u32[]{:S(2)}) async-start(f32[8,8,2880]{2,1,0:T(8,128)} %broadcast_in_dim.31), calls=%async_computation.2 | async-start | bytes 1507328 | tf_op jit(solution)/shard_map/all_to_all | solution.py:24
  82.3 39.8 %all-to-all-start.4 = ((bf16[4,90,1440]{1,0,2:T(4,128)(2,1)}), bf16[4,90,1440]{1,0,2:T(4,128)(2,1)S(1)}, u32[]{:S(2)}, u32[]{:S(2)}) async-start(bf16[4,90,1440]{1,0,2:T(4,128)(2,1)} %copy.157), calls=%async_computation.4 | async-start | bytes 2949120 | tf_op jit(solution)/shard_map/all_to_all | solution.py:70
  123.2 41.4 %all-to-all-start.6 = ((bf16[4,90,1440]{1,0,2:T(4,128)(2,1)}), bf16[4,90,1440]{1,0,2:T(4,128)(2,1)S(1)}, u32[]{:S(2)}, u32[]{:S(2)}) async-start(bf16[4,90,1440]{1,0,2:T(4,128)(2,1)} %copy.160), calls=%async_computation.6 | async-start | bytes 2949120 | tf_op jit(solution)/shard_map/all_to_all | solution.py:77
  137.3 39.2 %copy-start.13 = (f32[2,4,4]{2,1,0:T(4,128)S(1)}, f32[2,4,4]{2,1,0:T(4,128)}, u32[]{:S(2)}) copy-start(f32[2,4,4]{2,1,0:T(4,128)} %param.21) | copy-start | bytes 388
  137.3 39.2 %copy-start.14 = (s32[2,4,4]{2,1,0:T(4,128)S(1)}, s32[2,4,4]{2,1,0:T(4,128)}, u32[]{:S(2)}) copy-start(s32[2,4,4]{2,1,0:T(4,128)} %param.20) | copy-start | bytes 388
  137.3 40.9 %copy-start.12 = (f32[2880]{0:T(1024)S(1)}, f32[2880]{0:T(1024)}, u32[]{:S(2)}) copy-start(f32[2880]{0:T(1024)} %param.16) | copy-start | bytes 34564
  164.6 1.2 copy-start.6
  165.7 42.5 %all-to-all-start.8 = ((bf16[4,1440,90]{2,0,1:T(4,128)(2,1)}), bf16[4,1440,90]{2,0,1:T(4,128)(2,1)S(1)}, u32[]{:S(2)}, u32[]{:S(2)}) async-start(bf16[4,1440,90]{2,0,1:T(4,128)(2,1)} %copy.164), calls=%async_computation.8 | async-start | bytes 2949120 | tf_op jit(solution)/shard_map/all_to_all | solution.py:85
  208.2 16.3 %copy-start.5 = (bf16[4,1440,90]{2,0,1:T(4,128)(2,1)}, bf16[4,1440,90]{2,0,1:T(4,128)(2,1)S(1)}, u32[]{:S(2)}) copy-start(bf16[4,1440,90]{2,0,1:T(4,128)(2,1)S(1)} %all-to-all-done.8) | copy-start | bytes 3110404
  208.2 25.8 %all-to-all-start.3 = ((bf16[32,4,2880]{2,1,0:T(4,128)(2,1)}), bf16[32,4,2880]{2,1,0:T(4,128)(2,1)}, u32[]{:S(2)}, u32[]{:S(2)}) async-start(bf16[32,4,2880]{2,1,0:T(4,128)(2,1)} %copy.156), calls=%async_computation.3 | async-start | bytes 1507328 | tf_op jit(solution)/shard_map/all_to_all | solution.py:150
  234.1 23.7 %all-to-all-start.5 = ((bf16[32,90,180]{1,2,0:T(8,128)(2,1)}), bf16[32,90,180]{1,2,0:T(8,128)(2,1)S(1)}, u32[]{:S(2)}, u32[]{:S(2)}) async-start(bf16[32,90,180]{1,2,0:T(8,128)(2,1)} %bitcast.101), calls=%async_computation.5 | async-start | bytes 3014656 | tf_op jit(solution)/shard_map/all_to_all | solution.py:69
  258.9 23.5 %all-to-all-start.7 = ((bf16[32,90,180]{1,2,0:T(8,128)(2,1)}), bf16[32,90,180]{1,2,0:T(8,128)(2,1)}, u32[]{:S(2)}, u32[]{:S(2)}) async-start(bf16[32,90,180]{1,2,0:T(8,128)(2,1)} %bitcast.102), calls=%async_computation.7 | async-start | bytes 3014656 | tf_op jit(solution)/shard_map/all_to_all | solution.py:76
  282.5 24.1 %all-to-all-start.9 = ((bf16[32,180,90]{2,1,0:T(8,128)(2,1)}), bf16[32,180,90]{2,1,0:T(8,128)(2,1)}, u32[]{:S(2)}, u32[]{:S(2)}) async-start(bf16[32,180,90]{2,1,0:T(8,128)(2,1)} %bitcast.32), calls=%async_computation.9 | async-start | bytes 3014656 | tf_op jit(solution)/shard_map/all_to_all | solution.py:84
  303.0 2.1 copy-start.3
  303.0 2.1 copy-start.8
  361.2 20.2 %all-to-all-start.11 = ((bf16[32,4,360]{2,1,0:T(4,128)(2,1)}), bf16[32,4,360]{2,1,0:T(4,128)(2,1)S(1)}, u32[]{:S(2)}, u32[]{:S(2)}) async-start(bf16[32,4,360]{2,1,0:T(4,128)(2,1)} %copy.170), calls=%async_computation.11 | async-start | bytes 196608 | tf_op jit(solution)/shard_map/all_to_all | solution.py:161
  382.3 18.3 %all-to-all-start.12 = ((bf16[8,2,4,360]{3,2,1,0:T(4,128)(2,1)}), bf16[8,2,4,360]{3,2,1,0:T(4,128)(2,1)S(1)}, u32[]{:S(2)}, u32[]{:S(2)}) async-start(bf16[8,2,4,360]{3,2,1,0:T(4,128)(2,1)} %broadcast_in_dim.32), calls=%async_computation.12 | async-start | bytes 98304 | tf_op jit(solution)/shard_map/all_to_all | solution.py:24
  392.0 4.2 %copy-start.1 = (bf16[1,180,32,90]{3,2,1,0:T(8,128)(2,1)S(1)}, bf16[1,180,32,90]{3,2,1,0:T(8,128)(2,1)}, u32[]{:S(2)}) copy-start(bf16[1,180,32,90]{3,2,1,0:T(8,128)(2,1)} %copy.166) | copy-start | bytes 3110404
  (3 other events, 3.1 us)
where the time goes:
time: 403 us; the launch traced here: 401 us
  waiting for transfers between devices  156 us (39%)
  starting transfers between devices  96.5 us (24%)
  local copies, waits for them, and re-layouts  90.2 us (22%)
  blocking collectives  40.3 us (10%)
  matrix products  9.91 us (2%)
  other arithmetic  7.15 us (2%)
    all_to_all x1, blocking collectives, sum_at_owner(): tiles = lax.all_to_all(split_up(shard, dim, length), axis, 0, 0, tiled=True)  40.3 us
    unnamed x37, local copies, waits for them, and re-layouts  33.6 us
    all_to_all x1, waiting for transfers between devices, shards(): lax.all_to_all(w_down, 'cache', split_axis=1, concat_axis=0, tiled=True)  28.3 us
    all_to_all x1, waiting for transfers between devices, shards(): lax.all_to_all(w_gate, 'cache', split_axis=2, concat_axis=0, tiled=True)  27.8 us
    all_to_all x1, waiting for transfers between devices, shards(): lax.all_to_all(w_up, 'cache', split_axis=2, concat_axis=0, tiled=True)  27.3 us
    all_to_all x1, waiting for transfers between devices, shards(): lax.all_to_all(lax.all_to_all(w_gate, 'cache', split_axis=2, concat_axis=...  16.7 us
    all_to_all x1, waiting for transfers between devices, shards(): lax.all_to_all(lax.all_to_all(w_up, 'cache', split_axis=2, concat_axis=0,...  16.1 us
    all_to_all x2, waiting for transfers between devices, sent_to_all(): lax.all_to_all(jnp.broadcast_to(shard[None], (length, *shard.shape)), axi...  15.9 us
  transfers between devices with their start and end apart: 12, of which 10 were waited for; matrix products, arithmetic and copies ran while one was open for 14% of the time, Pallas kernels for 0%

commit v1 on v0

v1 whole, which is shorter than its diff:
```python
import math

import jax
import jax.numpy as jnp
from jax import lax
from jax.experimental import pallas as pl
from jax.experimental.pallas import tpu as pltpu
from jax.sharding import PartitionSpec as P

D = 2880
QH = 32
KVH = 4
HD = 64
TOP = 4
NEG = -1e30
BF = jnp.bfloat16
F32 = jnp.float32
NT = (((1,), (1,)), ((), ()))
PARAMS = pltpu.CompilerParams(vmem_limit_bytes=48 << 20)


def pack_kernel(gate_ref, up_ref, down_ref, out_ref):
    blocks, experts = out_ref.shape[0], out_ref.shape[1]
    depth = gate_ref.shape[0]
    half = depth // 2
    width = gate_ref.shape[2] // blocks
    for k in range(experts):
        gate = gate_ref[:, k, :]
        up = up_ref[:, k, :]
        down = down_ref[:, k, :]
        for c in range(blocks):
            cut = slice(c * width, (c + 1) * width)
            out_ref[c, k, 0:depth, :] = jnp.concatenate([gate[:, cut], up[:, cut]], axis=1)
            out_ref[c, k, depth : depth + half, :] = jnp.concatenate(
                [down[0:half, cut], down[half:depth, cut]], axis=1
            )


def pack(gate, up, down, blocks):
    depth, experts, width = gate.shape
    rows = -(-(depth + depth // 2) // 8) * 8
    return pl.pallas_call(
        pack_kernel,
        out_shape=jax.ShapeDtypeStruct((blocks, experts, rows, 2 * width // blocks), BF),
        compiler_params=PARAMS,
        name="pack",
    )(gate, up, down)


def attend_kernel(length_ref, base_ref, query_ref, key_ref, value_ref, out_ref):
    row = pl.program_id(0)
    heads = query_ref.shape[1]
    positions = key_ref.shape[1]
    scores = lax.dot_general(query_ref[0], key_ref[0], NT, preferred_element_type=F32)
    scores = scores * (1.0 / math.sqrt(HD))
    position = base_ref[0] + lax.broadcasted_iota(jnp.int32, (heads, positions), 1)
    step = (lax.broadcasted_iota(jnp.int32, (heads, positions), 0) >= heads // 2).astype(jnp.int32)
    visible = position < length_ref[row] + 1 + step
    highest = jnp.max(jnp.where(visible, scores, NEG), axis=-1, keepdims=True)
    highest = highest.astype(BF).astype(F32)
    weights = jnp.where(visible, jnp.exp(scores - highest), 0.0)
    mass = jnp.sum(weights, axis=-1, keepdims=True)
    wide = jnp.dot(weights.astype(BF), value_ref[0], preferred_element_type=F32)
    group = heads // (2 * KVH)
    own = (lax.broadcasted_iota(jnp.int32, (heads, HD), 0) // group) % KVH
    accum = jnp.zeros((heads, HD), F32)
    for h in range(KVH):
        accum = accum + jnp.where(own == h, wide[:, h * HD : (h + 1) * HD], 0.0)
    mass_high = mass.astype(BF).astype(F32)
    lane = lax.broadcasted_iota(jnp.int32, (heads, HD), 1)
    extra = jnp.where(lane == 0, highest, jnp.where(lane == 1, mass_high, jnp.where(lane == 2, mass - mass_high, 0.0)))
    out_ref[0] = jnp.concatenate([accum, extra], axis=1).astype(BF)


def attend(lengths, base, query, keys, values):
    rows, heads, width = query.shape
    positions = keys.shape[1]
    grid_spec = pltpu.PrefetchScalarGridSpec(
        num_scalar_prefetch=2,
        grid=(rows,),
        in_specs=[
            pl.BlockSpec((1, heads, width), lambda r, *_: (r, 0, 0)),
            pl.BlockSpec((1, positions, width), lambda r, *_: (r, 0, 0)),
            pl.BlockSpec((1, positions, width), lambda r, *_: (r, 0, 0)),
        ],
        out_specs=pl.BlockSpec((1, heads, 2 * HD), lambda r, *_: (r, 0, 0)),
    )
    return pl.pallas_call(
        attend_kernel,
        grid_spec=grid_spec,
        out_shape=jax.ShapeDtypeStruct((rows, heads, 2 * HD), BF),
        compiler_params=PARAMS,
        name="attend",
    )(lengths, base, query, keys, values)


def expert_kernel(slots_ref, weights_ref, out_ref, first_ref, second_ref):
    sources = weights_ref.shape[0]
    depth = first_ref.shape[0] // sources
    half = depth // 2
    rows = depth + half
    width = second_ref.shape[1]
    for j in range(sources):
        block = weights_ref[j]
        first_ref[j * depth : (j + 1) * depth, :] = block[0:depth]
        second_ref[j * depth : j * depth + half, :] = block[depth:rows, 0:width]
        second_ref[j * depth + half : (j + 1) * depth, :] = block[depth:rows, width : 2 * width]
    slots = slots_ref[...].reshape(out_ref.shape[0] * out_ref.shape[1], out_ref.shape[2])
    both = jnp.dot(slots, first_ref[...], preferred_element_type=F32)
    gate = both[:, 0:width]
    up = both[:, width : 2 * width]
    hidden = (gate * jax.nn.sigmoid(gate) * up).astype(BF)
    out = lax.dot_general(hidden, second_ref[...], NT, preferred_element_type=F32)
    out_ref[...] = out.astype(BF).reshape(out_ref.shape)


def expert(slots, weights):
    sources, width = weights.shape[0], weights.shape[2]
    depth = slots.shape[-1] // sources
    return pl.pallas_call(
        expert_kernel,
        out_shape=jax.ShapeDtypeStruct(slots.shape, BF),
        scratch_shapes=[
            pltpu.VMEM((sources * depth, width), BF),
            pltpu.VMEM((sources * depth, width // 2), BF),
        ],
        compiler_params=PARAMS,
        name="expert",
    )(slots, weights)


def owner_kernel(weights_ref, gate_ref, up_ref, down_ref, first_ref, second_ref):
    sources = weights_ref.shape[0]
    depth = first_ref.shape[0] // sources
    half = depth // 2
    rows = depth + half
    width = second_ref.shape[1]
    for j in range(sources):
        block = weights_ref[j]
        first_ref[j * depth : (j + 1) * depth, :] = block[0:depth]
        second_ref[j * depth : j * depth + half, :] = block[depth:rows, 0:width]
        second_ref[j * depth + half : (j + 1) * depth, :] = block[depth:rows, width : 2 * width]
    row = lax.broadcasted_iota(jnp.int32, (width, 2 * width), 0)
    lane = lax.broadcasted_iota(jnp.int32, (width, 2 * width), 1)
    first = first_ref[...]
    pick = (row == lane).astype(BF)
    gate_ref[...] = lax.dot_general(pick, first, NT, preferred_element_type=F32).astype(BF)
    pick = (row + width == lane).astype(BF)
    up_ref[...] = lax.dot_general(pick, first, NT, preferred_element_type=F32).astype(BF)
    row = lax.broadcasted_iota(jnp.int32, (width, width), 0)
    lane = lax.broadcasted_iota(jnp.int32, (width, width), 1)
    pick = (row == lane).astype(BF)
    down_ref[...] = lax.dot_general(pick, second_ref[...], NT, preferred_element_type=F32).astype(BF)


def owner(weights):
    sources, width = weights.shape[0], weights.shape[2]
    depth = D // sources
    shape = jax.ShapeDtypeStruct((width // 2, sources * depth), BF)
    return pl.pallas_call(
        owner_kernel,
        out_shape=(shape, shape, shape),
        scratch_shapes=[
            pltpu.VMEM((sources * depth, width), BF),
            pltpu.VMEM((sources * depth, width // 2), BF),
        ],
        compiler_params=PARAMS,
        name="owner",
    )(weights)


def shards(
    queries,
    k_cache,
    v_cache,
    lengths,
    w_out,
    norm_gain,
    w_gate,
    w_up,
    w_down,
    expert_ids,
    gate_weights,
):
    cache_count = lax.axis_size("cache")
    cache_place = lax.axis_index("cache")
    step_count = queries.shape[0]
    row_count, positions = k_cache.shape[0], k_cache.shape[1]
    group_size = QH // KVH

    packed = pack(
        jnp.transpose(w_gate, (1, 0, 2)),
        jnp.transpose(w_up, (1, 0, 2)),
        jnp.transpose(w_down, (2, 0, 1)),
        cache_count,
    )
    packed, queries = lax.optimization_barrier((packed, queries))
    moved = lax.all_to_all(packed, "cache", split_axis=0, concat_axis=0, tiled=True)

    query = queries.reshape(step_count, row_count, KVH, group_size, HD)
    query = jnp.transpose(query, (1, 0, 2, 3, 4))
    eye = jnp.eye(KVH, dtype=BF)
    query = query[:, :, :, :, None, :] * eye[None, None, :, None, :, None]
    query = query.reshape(row_count, step_count * QH, KVH * HD)
    base = (cache_place * positions).astype(jnp.int32).reshape(1)
    part = attend(lengths, base, query, k_cache, v_cache)
    parts = lax.all_gather(part, "cache", axis=0)
    own_heads = QH // cache_count
    parts = parts.reshape(cache_count, row_count, step_count, QH, 2 * HD)
    parts = lax.dynamic_slice_in_dim(parts, cache_place * own_heads, own_heads, 3).astype(F32)
    part_high = parts[..., HD : HD + 1]
    part_mass = parts[..., HD + 1 : HD + 2] + parts[..., HD + 2 : HD + 3]
    factor = jnp.exp(part_high - jnp.max(part_high, axis=0))
    own_out = jnp.sum(parts[..., 0:HD] * factor, axis=0) / jnp.sum(part_mass * factor, axis=0)
    own_rows = jnp.transpose(own_out.astype(BF), (1, 0, 2, 3)).reshape(step_count * row_count, own_heads * HD)
    projected = jnp.dot(own_rows, w_out, preferred_element_type=F32).astype(BF)
    attention = jnp.sum(lax.all_gather(projected, "cache", axis=0).astype(F32), axis=0)
    scale = lax.rsqrt(jnp.mean(attention * attention, axis=-1, keepdims=True) + 1e-05)
    normed = (attention * scale * norm_gain).astype(BF).reshape(step_count, row_count, D)

    experts_total = w_gate.shape[0] * cache_count
    capacity = max(2, (row_count * TOP + experts_total - 1) // experts_total)
    expert_range = jnp.arange(experts_total, dtype=jnp.int32)
    onehot = (expert_ids[..., None] == expert_range).astype(F32)
    chosen = jnp.sum(onehot, axis=2)
    gate_map = jnp.sum(onehot * gate_weights[..., None], axis=2)
    earlier = jnp.tril(jnp.ones((row_count, row_count), F32), -1)
    ranks = jnp.einsum("rq,sqe->sre", earlier, chosen, precision=lax.Precision.HIGHEST)
    slot_table = (ranks[..., None] == jnp.arange(capacity, dtype=F32)).astype(F32) * chosen[..., None]
    outgoing = jnp.einsum("srec,srd->escd", slot_table.astype(BF), normed, preferred_element_type=F32)
    outgoing = outgoing.astype(BF).reshape(experts_total, step_count * capacity, D)
    slots = lax.all_to_all(outgoing, "expert", split_axis=0, concat_axis=0, tiled=True)

    moved = moved.reshape(experts_total, moved.shape[2], moved.shape[3])
    arrived = lax.all_to_all(moved, "expert", split_axis=0, concat_axis=0, tiled=True)
    partial_out = expert(slots, arrived)
    returned = lax.all_to_all(partial_out, "expert", split_axis=0, concat_axis=0, tiled=True)
    arrived, partial_out = lax.optimization_barrier((arrived, partial_out))
    gate_owner, up_owner, down_owner = owner(arrived)

    returned = returned.reshape(experts_total, step_count, capacity, D)
    combined = jnp.einsum(
        "srec,escd->srd",
        slot_table * gate_map[..., None],
        returned.astype(F32),
        precision=lax.Precision.HIGHEST,
    )
    shares = lax.all_gather(combined.astype(BF), "cache", axis=0)
    total = jnp.sum(shares.astype(F32), axis=0) + attention.reshape(step_count, row_count, D)
    mixed = total.astype(BF)
    return (mixed, gate_owner.T[None], up_owner.T[None], down_owner[None])


def solution(mesh):
    return jax.shard_map(
        shards,
        mesh=mesh,
        in_specs=(
            P(None, "expert", None),
            P("expert", "cache", None),
            P("expert", "cache", None),
            P("expert"),
            P("cache", None),
            P(),
            P("cache", "expert", None),
            P("cache", "expert", None),
            P("cache", None, "expert"),
            P(None, "expert", None),
            P(None, "expert", None),
        ),
        out_specs=(
            P(None, "expert", None),
            P("expert", None, "cache"),
            P("expert", None, "cache"),
            P("expert", "cache", None),
        ),
        check_vma=False,
    )
```

time: 403 us -> 250 us (0.62)
  blocking collectives: 40.3 us -> 203 us
  waiting for transfers between devices: 156 us -> 6.14 us
  starting transfers between devices: 96.5 us -> 3.91 us
  local copies, waits for them, and re-layouts: 90.2 us -> 12.8 us
  Pallas kernels: 0 us -> 19.5 us
  matrix products: 9.91 us -> 1.58 us
  other arithmetic: 7.15 us -> 2.27 us
    all_to_all x12 -> x1, waiting for transfers between devices: 156 us -> 6.14 us  [shards(): lax.all_to_all(partial_out, 'expert', split_axis=0, concat_axis=0, tiled=...]
    all_to_all x1 -> x3, blocking collectives: 40.3 us -> 150 us  [the longest x1 67.5 us: shards(): lax.all_to_all(packed, 'cache', split_axis=0, concat_axis=0, tiled=True)]
    all_to_all x12 -> x1, starting transfers between devices: 96.5 us -> 3.91 us  [shards(): lax.all_to_all(partial_out, 'expert', split_axis=0, concat_axis=0, tiled=...]
    all_gather x0 -> x3, blocking collectives: none -> 52.5 us  [the longest x1 20 us: shards(): parts = lax.all_gather(part, 'cache', axis=0)]
    all_to_all x12 -> x0, local copies, waits for them, and re-layouts: 29.2 us -> none  [the longest x2 7.17 us: shards(): lax.all_to_all(lax.all_to_all(w_down, 'cache', split_axis=1, concat_axis=...]
    unnamed x37 -> x29, local copies, waits for them, and re-layouts: 33.6 us -> 11.4 us
    pallas_call x0 -> x4, Pallas kernels: none -> 19.5 us  [the longest x1 9.81 us: pack(): pl.pallas_call(pack_kernel, out_shape=jax.ShapeDtypeStruct((blocks, exper...]
    squeeze x3 -> x0, local copies, waits for them, and re-layouts: 12.7 us -> none  [the longest x1 4.42 us: shards(): gate_owner[0]]
  transfers between devices with their start and end apart: 12 -> 1, of which waited for: 10 -> 1; matrix products, arithmetic and copies ran while one was open for 14% -> 0% of each run, Pallas kernels for 0% -> 1%
where the time goes in v1:
time: 250 us
  blocking collectives  203 us (81%)
  Pallas kernels  19.5 us (8%)
  local copies, waits for them, and re-layouts  12.8 us (5%)
  waiting for transfers between devices  6.14 us (2%)
  starting transfers between devices  3.91 us (2%)
    all_to_all x1, blocking collectives, shards(): lax.all_to_all(packed, 'cache', split_axis=0, concat_axis=0, tiled=True)  67.5 us
    all_to_all x1, blocking collectives, shards(): lax.all_to_all(moved, 'expert', split_axis=0, concat_axis=0, tiled=True)  62.4 us
    all_to_all x1, blocking collectives, shards(): lax.all_to_all(outgoing, 'expert', split_axis=0, concat_axis=0, tiled=True)  20.2 us
    all_gather x1, blocking collectives, shards(): parts = lax.all_gather(part, 'cache', axis=0)  20 us
    all_gather x1, blocking collectives, shards(): shares = lax.all_gather(combined.astype(BF), 'cache', axis=0)  17.5 us
    all_gather x1, blocking collectives, shards(): lax.all_gather(projected, 'cache', axis=0).astype(F32)  15.1 us
    unnamed x29, local copies, waits for them, and re-layouts  11.4 us
    pallas_call x1, Pallas kernels, pack(): pl.pallas_call(pack_kernel, out_shape=jax.ShapeDtypeStruct((blocks, exper...  9.81 us
  transfers between devices with their start and end apart: 1, of which 1 were waited for; matrix products, arithmetic and copies ran while one was open for 0% of the time, Pallas kernels for 1%

profile of v1, /device:TPU:1, one launch (start us, length us, event | category | flops | bytes accessed | tf_op | source)
XLA Modules:
  0.0 249.8 jit_solution(4052211340889107599)
XLA Ops:
  0.9 1.4 copy-done.5
  2.3 1.2 copy-done.6
  3.5 1.2 copy-done.7
  4.7 9.8 %pack.1 = bf16[8,4,136,360]{3,2,1,0:T(8,128)(2,1)} custom-call(bf16[90,4,1440]{2,1,0:T(4,128)(2,1)S(1)} %bitcast.49, bf16[90,4,1440]{2,1,0:T(4,128)(2,1)S(1)} %bitcast.50, bf16[90,4,1440]{2,1,0:T(4,128)(2,1)S(1)} %bitcast.51), custom_call_target="tpu_custom_call" | custom-call | tf_op jit(solution)/shard_map/pack/pallas_call | solution.py:42
  15.0 1.6 copy-done.3
  16.6 1.6 copy-done.4
  18.2 3.5 %attend.1 = bf16[4,64,128]{2,1,0:T(8,128)(2,1)S(1)} custom-call(s32[4]{0:T(128)S(1)} %copy-done.8, s32[1]{0:T(128)} %bitcast.2.base_ref, bf16[4,64,256]{2,1,0:T(8,128)(2,1)S(1)} %broadcast_multiply_fusion.query_ref, bf16[4,1024,256]{2,1,0:T(8,128)(2,1)S(1)} %copy-done.3, bf16[4,1024,256]{2,1,0:T(8,128)(2,1)S(1)} %copy-done.4), custom_call_target="tpu_custom_call" | custom-call | tf_op jit(solution)/shard_map/attend/pallas_call | solution.py:88
  21.7 20.0 %all-gather = bf16[32,64,128]{2,1,0:T(8,128)(2,1)S(1)} all-gather(bf16[4,64,128]{2,1,0:T(8,128)(2,1)S(1)} %attend.1), channel_id=2, replica_groups=mesh['cache'=8,'expert'=32] {'cache'}, dimensions={0}, use_global_device_ids=true | all-gather | bytes 589824 | tf_op jit(solution)/shard_map/all_gather | solution.py:207
  41.8 0.7 copy.42
  42.9 0.6 fusion.1
  43.8 0.5 convolution_convert_fusion.1
  44.3 15.1 %all-gather.1 = bf16[64,2880]{1,0:T(8,128)(2,1)S(1)} all-gather(bf16[8,2880]{1,0:T(8,128)(2,1)S(1)} %convolution_convert_fusion.1), channel_id=3, replica_groups=mesh['cache'=8,'expert'=32] {'cache'}, dimensions={0}, use_global_device_ids=true | all-gather | bytes 414720 | tf_op jit(solution)/shard_map/all_gather | solution.py:217
  60.9 20.2 %all_to_all.20.slots_ref = bf16[32,4,2880]{2,1,0:T(4,128)(2,1)S(1)} all-to-all(bf16[32,4,2880]{2,1,0:T(4,128)(2,1)S(1)} %copy.40), channel_id=1, replica_groups=mesh['cache'=8,'expert'=32] {'expert'}, dimensions={0} | all-to-all | bytes 1474560 | tf_op jit(solution)/shard_map/all_to_all | solution.py:232
  81.1 67.5 %all_to_all.21 = bf16[8,4,136,360]{3,2,1,0:T(8,128)(2,1)S(1)} all-to-all(bf16[8,4,136,360]{3,2,1,0:T(8,128)(2,1)S(1)} %copy-done.9), channel_id=1, replica_groups=mesh['cache'=8,'expert'=32] {'cache'}, dimensions={0} | all-to-all | bytes 6266880 | tf_op jit(solution)/shard_map/all_to_all | solution.py:198
  148.6 62.4 %all_to_all.22.weights_ref = bf16[32,136,360]{2,1,0:T(8,128)(2,1)S(1)} all-to-all(bf16[32,136,360]{2,1,0:T(8,128)(2,1)S(1)} %bitcast.52), channel_id=1, replica_groups=mesh['cache'=8,'expert'=32] {'expert'}, dimensions={0} | all-to-all | bytes 6266880 | tf_op jit(solution)/shard_map/all_to_all | solution.py:235
  211.1 2.5 %expert.1 = bf16[32,4,2880]{2,1,0:T(4,128)(2,1)} custom-call(bf16[32,4,2880]{2,1,0:T(4,128)(2,1)S(1)} %all_to_all.20.slots_ref, bf16[32,136,360]{2,1,0:T(8,128)(2,1)S(1)} %all_to_all.22.weights_ref), custom_call_target="tpu_custom_call" | custom-call | tf_op jit(solution)/shard_map/expert/pallas_call | solution.py:120
  213.6 1.7 copy-done.1
  215.3 3.9 %all-to-all-start.3 = ((bf16[32,4,2880]{2,1,0:T(4,128)(2,1)}), bf16[32,4,2880]{2,1,0:T(4,128)(2,1)S(1)}, u32[]{:S(2)}, u32[]{:S(2)}) async-start(bf16[32,4,2880]{2,1,0:T(4,128)(2,1)} %expert.1), calls=%async_computation.3 | async-start | bytes 1507328 | tf_op jit(solution)/shard_map/all_to_all | solution.py:237
  219.2 1.9 copy-done.2
  221.1 3.6 %owner.1 = (bf16[180,2880]{1,0:T(8,128)(2,1)}, bf16[180,2880]{1,0:T(8,128)(2,1)}, bf16[180,2880]{1,0:T(8,128)(2,1)}) custom-call(bf16[32,136,360]{2,1,0:T(8,128)(2,1)S(1)} %copy-done.2), custom_call_target="tpu_custom_call" | custom-call | tf_op jit(solution)/shard_map/owner/pallas_call | solution.py:160
  224.8 6.1 %all-to-all-done.3 = bf16[32,4,2880]{2,1,0:T(4,128)(2,1)S(1)} async-done(((bf16[32,4,2880]{2,1,0:T(4,128)(2,1)}), bf16[32,4,2880]{2,1,0:T(4,128)(2,1)S(1)}, u32[]{:S(2)}, u32[]{:S(2)}) %all-to-all-start.3) | async-done | bytes 737312 | tf_op jit(solution)/shard_map/all_to_all | solution.py:237
  231.0 0.5 fusion
  231.5 17.5 %all-gather.2 = bf16[16,4,2880]{2,1,0:T(4,128)(2,1)S(1)} all-gather(bf16[2,4,2880]{2,1,0:T(4,128)(2,1)S(1)} %fusion), channel_id=4, replica_groups=mesh['cache'=8,'expert'=32] {'cache'}, dimensions={0}, use_global_device_ids=true | all-gather | bytes 414720 | tf_op jit(solution)/shard_map/all_gather | solution.py:248
  249.2 0.6 add_convert_fusion
  (49 shorter events, 3.1 us)
Async XLA Ops:
  0.6 43.2 %copy-start = (bf16[256,2880]{0,1:T(8,128)(2,1)S(1)}, bf16[256,2880]{0,1:T(8,128)(2,1)}, u32[]{:S(2)}) copy-start(bf16[256,2880]{0,1:T(8,128)(2,1)} %param.15) | copy-start | bytes 4423684
  0.9 1.4 copy-start.5
  2.3 1.2 copy-start.6
  3.5 1.2 copy-start.7
  4.7 9.8 %copy-start.10 = (bf16[2,4,2048]{2,1,0:T(4,128)(2,1)S(1)}, bf16[2,4,2048]{2,1,0:T(4,128)(2,1)}, u32[]{:S(2)}) copy-start(bf16[2,4,2048]{2,1,0:T(4,128)(2,1)} %param.11) | copy-start | bytes 98308
  4.7 10.3 %copy-start.8 = (s32[4]{0:T(128)S(1)}, s32[4]{0:T(128)}, u32[]{:S(2)}) copy-start(s32[4]{0:T(128)} %length_ref.1) | copy-start | bytes 52
  15.0 1.6 copy-start.3
  16.6 1.6 copy-start.4
  43.5 16.3 %copy-start.12 = (f32[2,4,4]{2,1,0:T(4,128)S(1)}, f32[2,4,4]{2,1,0:T(4,128)}, u32[]{:S(2)}) copy-start(f32[2,4,4]{2,1,0:T(4,128)} %param.21) | copy-start | bytes 388
  43.5 16.3 %copy-start.13 = (s32[2,4,4]{2,1,0:T(4,128)S(1)}, s32[2,4,4]{2,1,0:T(4,128)}, u32[]{:S(2)}) copy-start(s32[2,4,4]{2,1,0:T(4,128)} %param.20) | copy-start | bytes 388
  43.5 16.5 %copy-start.11 = (f32[2880]{0:T(1024)S(1)}, f32[2880]{0:T(1024)}, u32[]{:S(2)}) copy-start(f32[2880]{0:T(1024)} %param.16) | copy-start | bytes 34564
  60.0 21.1 %copy-start.9 = (bf16[8,4,136,360]{3,2,1,0:T(8,128)(2,1)S(1)}, bf16[8,4,136,360]{3,2,1,0:T(8,128)(2,1)}, u32[]{:S(2)}) copy-start(bf16[8,4,136,360]{3,2,1,0:T(8,128)(2,1)} %pack.1) | copy-start | bytes 9400324
  213.6 1.7 copy-start.1
  215.3 15.6 %all-to-all-start.3 = ((bf16[32,4,2880]{2,1,0:T(4,128)(2,1)}), bf16[32,4,2880]{2,1,0:T(4,128)(2,1)S(1)}, u32[]{:S(2)}, u32[]{:S(2)}) async-start(bf16[32,4,2880]{2,1,0:T(4,128)(2,1)} %expert.1), calls=%async_computation.3 | async-start | bytes 1507328 | tf_op jit(solution)/shard_map/all_to_all | solution.py:237
  219.2 1.9 copy-start.2

commit v2 on v1

v2 whole, which is shorter than its diff:
```python
import math

import jax
import jax.numpy as jnp
import numpy as np
from jax import lax
from jax.experimental import pallas as pl
from jax.experimental.pallas import tpu as pltpu
from jax.sharding import Mesh
from jax.sharding import PartitionSpec as P

D = 2880
QH = 32
KVH = 4
HD = 64
TOP = 4
NEG = -1e30
BF = jnp.bfloat16
F32 = jnp.float32
NT = (((1,), (1,)), ((), ()))
CACHE = ("zh", "core")
EXPERT = ("x", "zl", "y")
HI_STEPS = (2, 1, 3, 0)
PARAMS = pltpu.CompilerParams(vmem_limit_bytes=48 << 20)


def pack_kernel(place_ref, gate_ref, up_ref, down_ref, *refs):
    out_refs, block_ref, sems = refs[:-2], refs[-2], refs[-1]
    blocks, experts = block_ref.shape[0], block_ref.shape[1]
    depth = gate_ref.shape[0]
    half = depth // 2
    width = gate_ref.shape[2] // blocks
    for k in range(experts):
        gate = gate_ref[:, k, :]
        up = up_ref[:, k, :]
        down = down_ref[:, k, :]
        for c in range(blocks):
            cut = slice(c * width, (c + 1) * width)
            block_ref[c, k, 0:depth, :] = jnp.concatenate([gate[:, cut], up[:, cut]], axis=1)
            block_ref[c, k, depth : depth + half, :] = jnp.concatenate(
                [down[0:half, cut], down[half:depth, cut]], axis=1
            )
    copies = [
        pltpu.make_async_copy(block_ref.at[place_ref[i]], out_refs[i], sems.at[i]) for i in range(blocks)
    ]
    for copy in copies:
        copy.start()
    for copy in copies:
        copy.wait()


def pack(places, gate, up, down):
    depth, experts, width = gate.shape
    blocks = places.shape[0]
    rows = -(-(depth + depth // 2) // 8) * 8
    shape = (experts, rows, 2 * width // blocks)
    whole = pl.BlockSpec(gate.shape, lambda i, *_: (0, 0, 0))
    grid_spec = pltpu.PrefetchScalarGridSpec(
        num_scalar_prefetch=1,
        grid=(1,),
        in_specs=[whole, whole, whole],
        out_specs=[pl.BlockSpec(memory_space=pltpu.HBM)] * blocks,
        scratch_shapes=[pltpu.VMEM((blocks, *shape), BF), pltpu.SemaphoreType.DMA((blocks,))],
    )
    return pl.pallas_call(
        pack_kernel,
        grid_spec=grid_spec,
        out_shape=[jax.ShapeDtypeStruct(shape, BF)] * blocks,
        compiler_params=PARAMS,
        name="pack",
    )(places, gate, up, down)


def join_kernel(place_ref, *refs):
    in_refs, out_ref, sems = refs[:-2], refs[-2], refs[-1]
    experts = in_refs[0].shape[0]
    copies = [
        pltpu.make_async_copy(in_ref, out_ref.at[pl.ds(place_ref[i] * experts, experts)], sems.at[i])
        for i, in_ref in enumerate(in_refs)
    ]
    for copy in copies:
        copy.start()
    for copy in copies:
        copy.wait()


def join(places, blocks):
    experts, rows, width = blocks[0].shape
    count = len(blocks)
    anywhere = pl.BlockSpec(memory_space=pltpu.HBM)
    grid_spec = pltpu.PrefetchScalarGridSpec(
        num_scalar_prefetch=1,
        grid=(1,),
        in_specs=[anywhere] * count,
        out_specs=anywhere,
        scratch_shapes=[pltpu.SemaphoreType.DMA((count,))],
    )
    return pl.pallas_call(
        join_kernel,
        grid_spec=grid_spec,
        out_shape=jax.ShapeDtypeStruct((count * experts, rows, width), BF),
        compiler_params=PARAMS,
        name="join",
    )(places, *blocks)


def attend_kernel(length_ref, base_ref, query_ref, key_ref, value_ref, out_ref):
    row = pl.program_id(0)
    heads = query_ref.shape[1]
    positions = key_ref.shape[1]
    scores = lax.dot_general(query_ref[0], key_ref[0], NT, preferred_element_type=F32)
    scores = scores * (1.0 / math.sqrt(HD))
    position = base_ref[0] + lax.broadcasted_iota(jnp.int32, (heads, positions), 1)
    step = (lax.broadcasted_iota(jnp.int32, (heads, positions), 0) >= heads // 2).astype(jnp.int32)
    visible = position < length_ref[row] + 1 + step
    highest = jnp.max(jnp.where(visible, scores, NEG), axis=-1, keepdims=True)
    highest = highest.astype(BF).astype(F32)
    weights = jnp.where(visible, jnp.exp(scores - highest), 0.0)
    mass = jnp.sum(weights, axis=-1, keepdims=True)
    wide = jnp.dot(weights.astype(BF), value_ref[0], preferred_element_type=F32)
    group = heads // (2 * KVH)
    own = (lax.broadcasted_iota(jnp.int32, (heads, HD), 0) // group) % KVH
    accum = jnp.zeros((heads, HD), F32)
    for h in range(KVH):
        accum = accum + jnp.where(own == h, wide[:, h * HD : (h + 1) * HD], 0.0)
    mass_high = mass.astype(BF).astype(F32)
    lane = lax.broadcasted_iota(jnp.int32, (heads, HD), 1)
    extra = jnp.where(lane == 0, highest, jnp.where(lane == 1, mass_high, jnp.where(lane == 2, mass - mass_high, 0.0)))
    out_ref[0] = jnp.concatenate([accum, extra], axis=1).astype(BF)


def attend(lengths, base, query, keys, values):
    rows, heads, width = query.shape
    positions = keys.shape[1]
    grid_spec = pltpu.PrefetchScalarGridSpec(
        num_scalar_prefetch=2,
        grid=(rows,),
        in_specs=[
            pl.BlockSpec((1, heads, width), lambda r, *_: (r, 0, 0)),
            pl.BlockSpec((1, positions, width), lambda r, *_: (r, 0, 0)),
            pl.BlockSpec((1, positions, width), lambda r, *_: (r, 0, 0)),
        ],
        out_specs=pl.BlockSpec((1, heads, 2 * HD), lambda r, *_: (r, 0, 0)),
    )
    return pl.pallas_call(
        attend_kernel,
        grid_spec=grid_spec,
        out_shape=jax.ShapeDtypeStruct((rows, heads, 2 * HD), BF),
        compiler_params=PARAMS,
        name="attend",
    )(lengths, base, query, keys, values)


def stack(low_ref, high_ref, first_ref, second_ref):
    per = 4
    width = second_ref.shape[1]
    depth = first_ref.shape[0] // (2 * low_ref.shape[0])
    half = depth // 2
    rows = depth + half
    for i in range(low_ref.shape[0]):
        for z, ref in enumerate((low_ref, high_ref)):
            block = ref[i]
            at = ((i // per * 2 + z) * per + i % per) * depth
            first_ref[at : at + depth, :] = block[0:depth]
            second_ref[at : at + half, :] = block[depth:rows, 0:width]
            second_ref[at + half : at + depth, :] = block[depth:rows, width : 2 * width]


def stack_either(core_ref, zero_ref, one_ref, first_ref, second_ref):
    @pl.when(core_ref[0] == 0)
    def _():
        stack(zero_ref, one_ref, first_ref, second_ref)

    @pl.when(core_ref[0] != 0)
    def _():
        stack(one_ref, zero_ref, first_ref, second_ref)


def expert_kernel(core_ref, slots_ref, zero_ref, one_ref, out_ref, first_ref, second_ref):
    width = second_ref.shape[1]
    stack_either(core_ref, zero_ref, one_ref, first_ref, second_ref)
    slots = slots_ref[...].reshape(out_ref.shape[0] * out_ref.shape[1], out_ref.shape[2])
    both = jnp.dot(slots, first_ref[...], preferred_element_type=F32)
    gate = both[:, 0:width]
    up = both[:, width : 2 * width]
    hidden = (gate * jax.nn.sigmoid(gate) * up).astype(BF)
    out = lax.dot_general(hidden, second_ref[...], NT, preferred_element_type=F32)
    out_ref[...] = out.astype(BF).reshape(out_ref.shape)


def whole_spec(shape):
    zeros = (0,) * len(shape)
    return pl.BlockSpec(shape, lambda i, *_: zeros)


def expert(core, slots, zero, one):
    width = zero.shape[2]
    grid_spec = pltpu.PrefetchScalarGridSpec(
        num_scalar_prefetch=1,
        grid=(1,),
        in_specs=[whole_spec(slots.shape), whole_spec(zero.shape), whole_spec(one.shape)],
        out_specs=whole_spec(slots.shape),
        scratch_shapes=[pltpu.VMEM((D, width), BF), pltpu.VMEM((D, width // 2), BF)],
    )
    return pl.pallas_call(
        expert_kernel,
        grid_spec=grid_spec,
        out_shape=jax.ShapeDtypeStruct(slots.shape, BF),
        compiler_params=PARAMS,
        name="expert",
    )(core, slots, zero, one)


def owner_kernel(core_ref, zero_ref, one_ref, gate_ref, up_ref, down_ref, first_ref, second_ref):
    width = second_ref.shape[1]
    stack_either(core_ref, zero_ref, one_ref, first_ref, second_ref)
    row = lax.broadcasted_iota(jnp.int32, (width, 2 * width), 0)
    lane = lax.broadcasted_iota(jnp.int32, (width, 2 * width), 1)
    first = first_ref[...]
    pick = (row == lane).astype(BF)
    gate_ref[...] = lax.dot_general(pick, first, NT, preferred_element_type=F32).astype(BF)
    pick = (row + width == lane).astype(BF)
    up_ref[...] = lax.dot_general(pick, first, NT, preferred_element_type=F32).astype(BF)
    row = lax.broadcasted_iota(jnp.int32, (width, width), 0)
    lane = lax.broadcasted_iota(jnp.int32, (width, width), 1)
    pick = (row == lane).astype(BF)
    down_ref[...] = lax.dot_general(pick, second_ref[...], NT, preferred_element_type=F32).astype(BF)


def owner(core, zero, one):
    width = zero.shape[2]
    shape = jax.ShapeDtypeStruct((width // 2, D), BF)
    grid_spec = pltpu.PrefetchScalarGridSpec(
        num_scalar_prefetch=1,
        grid=(1,),
        in_specs=[whole_spec(zero.shape), whole_spec(one.shape)],
        out_specs=[whole_spec(shape.shape)] * 3,
        scratch_shapes=[pltpu.VMEM((D, width), BF), pltpu.VMEM((D, width // 2), BF)],
    )
    return pl.pallas_call(
        owner_kernel,
        grid_spec=grid_spec,
        out_shape=(shape, shape, shape),
        compiler_params=PARAMS,
        name="owner",
    )(core, zero, one)


def along_z(hi, core):
    shape = (4, 2, 4, 2, 4)
    pairs = []
    for zh, co, x, zl, y in np.ndindex(shape):
        target = ((zh + hi) % 4, (zl + core) % 2, x, co, y)
        pairs.append((int(np.ravel_multi_index((zh, co, x, zl, y), shape)), int(np.ravel_multi_index(target, shape))))
    return pairs


def shards(
    queries,
    k_cache,
    v_cache,
    lengths,
    w_out,
    norm_gain,
    w_gate,
    w_up,
    w_down,
    expert_ids,
    gate_weights,
):
    cache_count = lax.axis_size(CACHE)
    cache_place = lax.axis_index(CACHE)
    step_count = queries.shape[0]
    row_count, positions = k_cache.shape[0], k_cache.shape[1]
    group_size = QH // KVH

    zh, core, zl = lax.axis_index("zh"), lax.axis_index("core"), lax.axis_index("zl")
    places = [(zh + hi) % 4 * 2 + (zl + c) % 2 for c in range(2) for hi in HI_STEPS]
    packed = pack(
        jnp.stack(places).astype(jnp.int32),
        jnp.transpose(w_gate, (1, 0, 2)),
        jnp.transpose(w_up, (1, 0, 2)),
        jnp.transpose(w_down, (2, 0, 1)),
    )
    packed, queries = lax.optimization_barrier((packed, queries))
    moved = [
        lax.ppermute(packed[c * 4 + i], CACHE + EXPERT, along_z(hi, c))
        for c in range(2)
        for i, hi in enumerate(HI_STEPS)
    ]

    query = queries.reshape(step_count, row_count, KVH, group_size, HD)
    query = jnp.transpose(query, (1, 0, 2, 3, 4))
    eye = jnp.eye(KVH, dtype=BF)
    query = query[:, :, :, :, None, :] * eye[None, None, :, None, :, None]
    query = query.reshape(row_count, step_count * QH, KVH * HD)
    base = (cache_place * positions).astype(jnp.int32).reshape(1)
    part = attend(lengths, base, query, k_cache, v_cache)
    parts = lax.all_gather(part, CACHE, axis=0)
    parts, moved[0:3] = lax.optimization_barrier((parts, moved[0:3]))
    own_heads = QH // cache_count
    parts = parts.reshape(cache_count, row_count, step_count, QH, 2 * HD)
    parts = lax.dynamic_slice_in_dim(parts, cache_place * own_heads, own_heads, 3).astype(F32)
    part_high = parts[..., HD : HD + 1]
    part_mass = parts[..., HD + 1 : HD + 2] + parts[..., HD + 2 : HD + 3]
    factor = jnp.exp(part_high - jnp.max(part_high, axis=0))
    own_out = jnp.sum(parts[..., 0:HD] * factor, axis=0) / jnp.sum(part_mass * factor, axis=0)
    own_rows = jnp.transpose(own_out.astype(BF), (1, 0, 2, 3)).reshape(step_count * row_count, own_heads * HD)
    projected = jnp.dot(own_rows, w_out, preferred_element_type=F32).astype(BF)
    projected = lax.all_gather(projected, CACHE, axis=0)
    projected, moved[3:5] = lax.optimization_barrier((projected, moved[3:5]))
    attention = jnp.sum(projected.astype(F32), axis=0)
    scale = lax.rsqrt(jnp.mean(attention * attention, axis=-1, keepdims=True) + 1e-05)
    normed = (attention * scale * norm_gain).astype(BF).reshape(step_count, row_count, D)

    experts_total = w_gate.shape[0] * cache_count
    capacity = max(2, (row_count * TOP + experts_total - 1) // experts_total)
    expert_range = jnp.arange(experts_total, dtype=jnp.int32)
    onehot = (expert_ids[..., None] == expert_range).astype(F32)
    chosen = jnp.sum(onehot, axis=2)
    gate_map = jnp.sum(onehot * gate_weights[..., None], axis=2)
    earlier = jnp.tril(jnp.ones((row_count, row_count), F32), -1)
    ranks = jnp.einsum("rq,sqe->sre", earlier, chosen, precision=lax.Precision.HIGHEST)
    slot_table = (ranks[..., None] == jnp.arange(capacity, dtype=F32)).astype(F32) * chosen[..., None]
    outgoing = jnp.einsum("srec,srd->escd", slot_table.astype(BF), normed, preferred_element_type=F32)
    outgoing = outgoing.astype(BF).reshape(experts_total, step_count * capacity, D)
    slots = lax.all_to_all(outgoing, EXPERT, split_axis=0, concat_axis=0, tiled=True)

    turns = jnp.stack([(zh - hi) % 4 for hi in HI_STEPS]).astype(jnp.int32)
    zero = join(turns, moved[0:4])
    zero, slots, moved[5:7] = lax.optimization_barrier((zero, slots, moved[5:7]))
    zero = lax.all_to_all(zero, ("x", "y"), split_axis=0, concat_axis=0, tiled=True)
    one = lax.all_to_all(join(turns, moved[4:8]), ("x", "y"), split_axis=0, concat_axis=0, tiled=True)
    core = core.astype(jnp.int32).reshape(1)
    partial_out = expert(core, slots, zero, one)
    returned = lax.all_to_all(partial_out, EXPERT, split_axis=0, concat_axis=0, tiled=True)
    zero, one, partial_out = lax.optimization_barrier((zero, one, partial_out))
    gate_owner, up_owner, down_owner = owner(core, zero, one)

    returned = returned.reshape(experts_total, step_count, capacity, D)
    combined = jnp.einsum(
        "srec,escd->srd",
        slot_table * gate_map[..., None],
        returned.astype(F32),
        precision=lax.Precision.HIGHEST,
    )
    shares = lax.all_gather(combined.astype(BF), CACHE, axis=0)
    total = jnp.sum(shares.astype(F32), axis=0) + attention.reshape(step_count, row_count, D)
    mixed = total.astype(BF)
    return (mixed, gate_owner.T[None], up_owner.T[None], down_owner[None])


def solution(mesh):
    return jax.shard_map(
        shards,
        mesh=Mesh(mesh.devices.reshape(4, 2, 4, 2, 4), CACHE + EXPERT),
        in_specs=(
            P(None, EXPERT, None),
            P(EXPERT, CACHE, None),
            P(EXPERT, CACHE, None),
            P(EXPERT),
            P(CACHE, None),
            P(),
            P(CACHE, EXPERT, None),
            P(CACHE, EXPERT, None),
            P(CACHE, None, EXPERT),
            P(None, EXPERT, None),
            P(None, EXPERT, None),
        ),
        out_specs=(
            P(None, EXPERT, None),
            P(EXPERT, None, CACHE),
            P(EXPERT, None, CACHE),
            P(EXPERT, CACHE, None),
        ),
        check_vma=False,
    )
```

time: 250 us -> 243 us (0.972)
  blocking collectives: 203 us -> 110 us
  starting transfers between devices: 3.91 us -> 43.1 us
  waiting for transfers between devices: 6.14 us -> 38.3 us
  local copies, waits for them, and re-layouts: 12.8 us -> 19.6 us
  Pallas kernels: 19.5 us -> 25.5 us
    all_to_all x3 -> x1, blocking collectives: 150 us -> 24.8 us  [shards(): lax.all_to_all(join(turns, moved[4:8]), ('x', 'y'), split_axis=0, concat_...]
    all_gather x3, blocking collectives: 52.5 us -> 85.4 us  [the longest x1 47.8 us: shards(): parts = lax.all_gather(part, CACHE, axis=0)]
    ppermute x0 -> x8, waiting for transfers between devices: none -> 23.5 us  [shards(): lax.ppermute(packed[c * 4 + i], CACHE + EXPERT, along_z(hi, c))]
    ppermute x0 -> x8, starting transfers between devices: none -> 22.3 us  [shards(): lax.ppermute(packed[c * 4 + i], CACHE + EXPERT, along_z(hi, c))]
    all_to_all x1 -> x3, starting transfers between devices: 3.91 us -> 20.8 us  [the longest x1 9.69 us: shards(): lax.all_to_all(outgoing, EXPERT, split_axis=0, concat_axis=0, tiled=True)]
    all_to_all x1 -> x3, waiting for transfers between devices: 6.14 us -> 14.9 us  [the longest x1 10.7 us: shards(): lax.all_to_all(zero, ('x', 'y'), split_axis=0, concat_axis=0, tiled=True)]
    pallas_call x3 -> x5, Pallas kernels: 16 us -> 22 us  [the longest x1 11.2 us: pack(): pl.pallas_call(pack_kernel, grid_spec=grid_spec, out_shape=[jax.ShapeDtyp...]
    unnamed x29 -> x50, local copies, waits for them, and re-layouts: 11.4 us -> 15.8 us
  transfers between devices with their start and end apart: 1 -> 11, of which waited for: 1 -> 4; matrix products, arithmetic and copies ran while one was open for 0% -> 1% of each run, Pallas kernels for 1% -> 5%
where the time goes in v2:
time: 243 us; the launch traced here: 242 us
  blocking collectives  110 us (45%)
  starting transfers between devices  43.1 us (18%)
  waiting for transfers between devices  38.3 us (16%)
  Pallas kernels  25.5 us (10%)
  local copies, waits for them, and re-layouts  19.6 us (8%)
  other arithmetic  2.66 us (1%)
    all_gather x1, blocking collectives, shards(): parts = lax.all_gather(part, CACHE, axis=0)  47.8 us
    all_to_all x1, blocking collectives, shards(): lax.all_to_all(join(turns, moved[4:8]), ('x', 'y'), split_axis=0, concat_...  24.8 us
    ppermute x8, waiting for transfers between devices, shards(): lax.ppermute(packed[c * 4 + i], CACHE + EXPERT, along_z(hi, c))  23.5 us
    ppermute x8, starting transfers between devices, shards(): lax.ppermute(packed[c * 4 + i], CACHE + EXPERT, along_z(hi, c))  22.3 us
    all_gather x1, blocking collectives, shards(): shares = lax.all_gather(combined.astype(BF), CACHE, axis=0)  22.2 us
    unnamed x50, local copies, waits for them, and re-layouts  15.8 us
    all_gather x1, blocking collectives, shards(): projected = lax.all_gather(projected, CACHE, axis=0)  15.4 us
    pallas_call x1, Pallas kernels, pack(): pl.pallas_call(pack_kernel, grid_spec=grid_spec, out_shape=[jax.ShapeDtyp...  11.2 us
  transfers between devices with their start and end apart: 11, of which 4 were waited for; matrix products, arithmetic and copies ran while one was open for 1% of the time, Pallas kernels for 5%

profile of v2, /device:TPU:1, one launch (start us, length us, event | category | flops | bytes accessed | tf_op | source)
XLA Modules:
  0.0 242.0 jit_solution(16653922947762030325)
XLA Ops:
  3.4 11.2 %pack.1 = (bf16[4,136,360]{2,1,0:T(8,128)(2,1)}, bf16[4,136,360]{2,1,0:T(8,128)(2,1)}, bf16[4,136,360]{2,1,0:T(8,128)(2,1)}, bf16[4,136,360]{2,1,0:T(8,128)(2,1)...) custom-call(s32[8]{0:T(128)S(1)} %stack.55.place_ref, ...), custom_call_target="tpu_custom_call" | custom-call | tf_op jit(solution)/shard_map/pack/pallas_call | solution.py:65
  16.9 7.9 %collective-permute-start = (bf16[4,136,360]{2,1,0:T(8,128)(2,1)}, bf16[4,136,360]{2,1,0:T(8,128)(2,1)S(1)}, u32[]{:S(2)}, u32[]{:S(2)}) collective-permute-start(bf16[4,136,360]{2,1,0:T(8,128)(2,1)} %get-tuple-element.46), channel_id=1, source_target_pairs={{0,128},{1,129},{2,130},{3,131},{4,160},{5,161},{6,162},{7,163},{8... | collective-permute-start | bytes 1175048 | tf_op jit(solution)/shard_map/ppermute | solution.py:287
  26.1 1.6 collective-permute-start.2
  27.7 4.1 %collective-permute-start.3 = (bf16[4,136,360]{2,1,0:T(8,128)(2,1)}, bf16[4,136,360]{2,1,0:T(8,128)(2,1)}, u32[]{:S(2)}, u32[]{:S(2)}) collective-permute-start(bf16[4,136,360]{2,1,0:T(8,128)(2,1)} %get-tuple-element.53), channel_id=1, source_target_pairs={{0,0},{1,1},{2,2},{3,3},{4,32},{5,33},{6,34},{7,35},{8,8},{9,9},{1... | collective-permute-start | bytes 1175048 | tf_op jit(solution)/shard_map/ppermute | solution.py:287
  31.8 1.8 collective-permute-start.4
  35.0 1.6 copy-done.8
  36.6 1.6 copy-done.9
  38.1 3.5 %attend.1 = bf16[4,64,128]{2,1,0:T(8,128)(2,1)S(1)} custom-call(s32[4]{0:T(128)S(1)} %copy-done.14, s32[1]{0:T(128)} %bitcast.7.base_ref, bf16[4,64,256]{2,1,0:T(8,128)(2,1)S(1)} %broadcast_multiply_fusion.query_ref, bf16[4,1024,256]{2,1,0:T(8,128)(2,1)S(1)} %copy-done.8, bf16[4,1024,256]{2,1,0:T(8,128)(2,1)S(1)} %copy-done.9), custom_call_target="tpu_custom_call" | custom-call | tf_op jit(solution)/shard_map/attend/pallas_call | solution.py:145
  41.9 47.8 %all-gather = bf16[32,64,128]{2,1,0:T(8,128)(2,1)S(1)} all-gather(bf16[4,64,128]{2,1,0:T(8,128)(2,1)S(1)} %attend.1), channel_id=2, replica_groups=mesh['zh'=4,'core'=2,'x'=4,'zl'=2,'y'=4] {'zh','core'}, dimensions={0}, use_global_device_ids=true | all-gather | bytes 589824 | tf_op jit(solution)/shard_map/all_gather | solution.py:299
  91.6 15.4 %all-gather.1 = bf16[64,2880]{1,0:T(8,128)(2,1)S(1)} all-gather(bf16[8,2880]{1,0:T(8,128)(2,1)S(1)} %convolution_convert_fusion.1), channel_id=3, replica_groups=mesh['zh'=4,'core'=2,'x'=4,'zl'=2,'y'=4] {'zh','core'}, dimensions={0}, use_global_device_ids=true | all-gather | bytes 414720 | tf_op jit(solution)/shard_map/all_gather | solution.py:310
  109.0 9.7 %all-to-all-start = ((bf16[32,4,2880]{2,1,0:T(4,128)(2,1)}), bf16[32,4,2880]{2,1,0:T(4,128)(2,1)S(1)}, u32[]{:S(2)}, u32[]{:S(2)}) async-start(bf16[32,4,2880]{2,1,0:T(4,128)(2,1)} %copy.40), calls=%async_computation | async-start | bytes 1507328 | tf_op jit(solution)/shard_map/all_to_all | solution.py:327
  119.9 3.2 %collective-permute-start.6 = (bf16[4,136,360]{2,1,0:T(8,128)(2,1)}, bf16[4,136,360]{2,1,0:T(8,128)(2,1)}, u32[]{:S(2)}, u32[]{:S(2)}) collective-permute-start(bf16[4,136,360]{2,1,0:T(8,128)(2,1)} %copy-done.16), channel_id=1, source_target_pairs={{0,224},{1,225},{2,226},{3,227},{4,192},{5,193},{6,194},{7,195},{8... | collective-permute-start | bytes 1175048 | tf_op jit(solution)/shard_map/ppermute | solution.py:287
  123.1 2.2 join.2
  126.6 18.1 %collective-permute-done.5.refs_1_ = bf16[4,136,360]{2,1,0:T(8,128)(2,1)} collective-permute-done((bf16[4,136,360]{2,1,0:T(8,128)(2,1)}, bf16[4,136,360]{2,1,0:T(8,128)(2,1)}, u32[]{:S(2)}, u32[]{:S(2)}) %collective-permute-start.5) | collective-permute-done | bytes 391712 | tf_op jit(solution)/shard_map/ppermute | solution.py:287
  145.6 6.3 %all-to-all-start.1 = ((bf16[16,136,360]{2,1,0:T(8,128)(2,1)}), bf16[16,136,360]{2,1,0:T(8,128)(2,1)S(1)}, u32[]{:S(2)}, u32[]{:S(2)}) async-start(bf16[16,136,360]{2,1,0:T(8,128)(2,1)} %copy-done.3), calls=%async_computation.1 | async-start | bytes 3342336 | tf_op jit(solution)/shard_map/all_to_all | solution.py:332
  153.2 5.3 %collective-permute-done.7.refs_3_ = bf16[4,136,360]{2,1,0:T(8,128)(2,1)S(1)} collective-permute-done((bf16[4,136,360]{2,1,0:T(8,128)(2,1)}, bf16[4,136,360]{2,1,0:T(8,128)(2,1)S(1)}, u32[]{:S(2)}, u32[]{:S(2)}) %collective-permute-start.7) | collective-permute-done | bytes 391712 | tf_op jit(solution)/shard_map/ppermute | solution.py:287
  159.5 1.9 join.3
  162.6 10.7 %all-to-all-done.1.zero_ref = bf16[16,136,360]{2,1,0:T(8,128)(2,1)S(1)} async-done(((bf16[16,136,360]{2,1,0:T(8,128)(2,1)}), bf16[16,136,360]{2,1,0:T(8,128)(2,1)S(1)}, u32[]{:S(2)}, u32[]{:S(2)}) %all-to-all-start.1) | async-done | bytes 1566752 | tf_op jit(solution)/shard_map/all_to_all | solution.py:332
  173.3 24.8 %all_to_all.20.one_ref = bf16[16,136,360]{2,1,0:T(8,128)(2,1)S(1)} all-to-all(bf16[16,136,360]{2,1,0:T(8,128)(2,1)} %copy-done.4), channel_id=1, replica_groups=mesh['zh'=4,'core'=2,'x'=4,'zl'=2,'y'=4] {'x','y'}, dimensions={0} | all-to-all | bytes 3133440 | tf_op jit(solution)/shard_map/all_to_all | solution.py:333
  198.1 2.3 expert.1
  202.5 4.8 %all-to-all-start.3 = ((bf16[32,4,2880]{2,1,0:T(4,128)(2,1)}), bf16[32,4,2880]{2,1,0:T(4,128)(2,1)}, u32[]{:S(2)}, u32[]{:S(2)}) async-start(bf16[32,4,2880]{2,1,0:T(4,128)(2,1)} %copy-done.7), calls=%async_computation.3 | async-start | bytes 1507328 | tf_op jit(solution)/shard_map/all_to_all | solution.py:336
  208.8 4.3 %owner.1 = (bf16[180,2880]{1,0:T(8,128)(2,1)}, bf16[180,2880]{1,0:T(8,128)(2,1)}, bf16[180,2880]{1,0:T(8,128)(2,1)}) custom-call(s32[1]{0:T(128)} %bitcast.2.core_ref, bf16[16,136,360]{2,1,0:T(8,128)(2,1)S(1)} %all-to-all-done.1.zero_ref, bf16[16,136,360]{2,1,0:T(8,128)(2,1)S(1)} %copy-done.2), custom_call_target="tpu_custom_call" | custom-call | tf_op jit(solution)/shard_map/owner/pallas_call | solution.py:240
  213.1 4.2 %all-to-all-done.3 = bf16[32,4,2880]{2,1,0:T(4,128)(2,1)} async-done(((bf16[32,4,2880]{2,1,0:T(4,128)(2,1)}), bf16[32,4,2880]{2,1,0:T(4,128)(2,1)}, u32[]{:S(2)}, u32[]{:S(2)}) %all-to-all-start.3) | async-done | bytes 737312 | tf_op jit(solution)/shard_map/all_to_all | solution.py:336
  218.9 22.2 %all-gather.2 = bf16[16,4,2880]{2,1,0:T(4,128)(2,1)S(1)} all-gather(bf16[2,4,2880]{2,1,0:T(4,128)(2,1)S(1)} %fusion), channel_id=4, replica_groups=mesh['zh'=4,'core'=2,'x'=4,'zl'=2,'y'=4] {'zh','core'}, dimensions={0}, use_global_device_ids=true | all-gather | bytes 414720 | tf_op jit(solution)/shard_map/all_gather | solution.py:347
  (92 shorter events, 24.5 us)
Async XLA Ops:
  0.6 90.5 %copy-start = (bf16[256,2880]{0,1:T(8,128)(2,1)S(1)}, bf16[256,2880]{0,1:T(8,128)(2,1)}, u32[]{:S(2)}) copy-start(bf16[256,2880]{0,1:T(8,128)(2,1)} %param.15) | copy-start | bytes 4423684
  3.4 30.8 %copy-start.20 = (bf16[2,4,2048]{2,1,0:T(4,128)(2,1)S(1)}, bf16[2,4,2048]{2,1,0:T(4,128)(2,1)}, u32[]{:S(2)}) copy-start(bf16[2,4,2048]{2,1,0:T(4,128)(2,1)} %param.11) | copy-start | bytes 98308
  3.4 31.5 %copy-start.22 = (f32[2,4,4]{2,1,0:T(4,128)S(1)}, f32[2,4,4]{2,1,0:T(4,128)}, u32[]{:S(2)}) copy-start(f32[2,4,4]{2,1,0:T(4,128)} %param.21) | copy-start | bytes 388
  3.4 31.5 %copy-start.23 = (s32[2,4,4]{2,1,0:T(4,128)S(1)}, s32[2,4,4]{2,1,0:T(4,128)}, u32[]{:S(2)}) copy-start(s32[2,4,4]{2,1,0:T(4,128)} %param.20) | copy-start | bytes 388
  3.4 31.6 %copy-start.14 = (s32[4]{0:T(128)S(1)}, s32[4]{0:T(128)}, u32[]{:S(2)}) copy-start(s32[4]{0:T(128)} %length_ref.1) | copy-start | bytes 52
  16.9 72.8 %collective-permute-start = (bf16[4,136,360]{2,1,0:T(8,128)(2,1)}, bf16[4,136,360]{2,1,0:T(8,128)(2,1)S(1)}, u32[]{:S(2)}, u32[]{:S(2)}) collective-permute-start(bf16[4,136,360]{2,1,0:T(8,128)(2,1)} %get-tuple-element.46), channel_id=1, source_target_pairs={{0,128},{1,129},{2,130},{3,131},{4,160},{5,161},{6,162},{7,163},{8... | collective-permute-start | bytes 1175048 | tf_op jit(solution)/shard_map/ppermute | solution.py:287
  24.7 65.0 %collective-permute-start.1 = (bf16[4,136,360]{2,1,0:T(8,128)(2,1)}, bf16[4,136,360]{2,1,0:T(8,128)(2,1)S(1)}, u32[]{:S(2)}, u32[]{:S(2)}) collective-permute-start(bf16[4,136,360]{2,1,0:T(8,128)(2,1)} %get-tuple-element.47), channel_id=1, source_target_pairs={{0,64},{1,65},{2,66},{3,67},{4,96},{5,97},{6,98},{7,99},{8,72},{9,... | collective-permute-start | bytes 1175048 | tf_op jit(solution)/shard_map/ppermute | solution.py:287
  26.1 63.6 %collective-permute-start.2 = (bf16[4,136,360]{2,1,0:T(8,128)(2,1)}, bf16[4,136,360]{2,1,0:T(8,128)(2,1)S(1)}, u32[]{:S(2)}, u32[]{:S(2)}) collective-permute-start(bf16[4,136,360]{2,1,0:T(8,128)(2,1)} %get-tuple-element.48), channel_id=1, source_target_pairs={{0,192},{1,193},{2,194},{3,195},{4,224},{5,225},{6,226},{7,227},{8... | collective-permute-start | bytes 1175048 | tf_op jit(solution)/shard_map/ppermute | solution.py:287
  27.7 79.3 %collective-permute-start.3 = (bf16[4,136,360]{2,1,0:T(8,128)(2,1)}, bf16[4,136,360]{2,1,0:T(8,128)(2,1)}, u32[]{:S(2)}, u32[]{:S(2)}) collective-permute-start(bf16[4,136,360]{2,1,0:T(8,128)(2,1)} %get-tuple-element.53), channel_id=1, source_target_pairs={{0,0},{1,1},{2,2},{3,3},{4,32},{5,33},{6,34},{7,35},{8,8},{9,9},{1... | collective-permute-start | bytes 1175048 | tf_op jit(solution)/shard_map/ppermute | solution.py:287
  31.8 75.2 %collective-permute-start.4 = (bf16[4,136,360]{2,1,0:T(8,128)(2,1)}, bf16[4,136,360]{2,1,0:T(8,128)(2,1)S(1)}, u32[]{:S(2)}, u32[]{:S(2)}) collective-permute-start(bf16[4,136,360]{2,1,0:T(8,128)(2,1)} %get-tuple-element.54), channel_id=1, source_target_pairs={{0,160},{1,161},{2,162},{3,163},{4,128},{5,129},{6,130},{7,131},{8... | collective-permute-start | bytes 1175048 | tf_op jit(solution)/shard_map/ppermute | solution.py:287
  35.0 1.6 copy-start.8
  36.5 1.6 copy-start.9
  38.1 3.5 %copy-start.24 = (s32[4]{0:T(128)S(1)}, s32[4]{0:T(128)}, u32[]{:S(2)}) copy-start(s32[4]{0:T(128)} %iota_add_fusion) | copy-start | bytes 52
  90.7 16.6 %copy-start.21 = (f32[2880]{0:T(1024)S(1)}, f32[2880]{0:T(1024)}, u32[]{:S(2)}) copy-start(f32[2880]{0:T(1024)} %param.16) | copy-start | bytes 34564
  107.0 2.0 copy-start.12
  107.1 1.9 copy-start.18
  109.0 35.7 %all-to-all-start = ((bf16[32,4,2880]{2,1,0:T(4,128)(2,1)}), bf16[32,4,2880]{2,1,0:T(4,128)(2,1)S(1)}, u32[]{:S(2)}, u32[]{:S(2)}) async-start(bf16[32,4,2880]{2,1,0:T(4,128)(2,1)} %copy.40), calls=%async_computation | async-start | bytes 1507328 | tf_op jit(solution)/shard_map/all_to_all | solution.py:327
  118.7 26.0 %collective-permute-start.5 = (bf16[4,136,360]{2,1,0:T(8,128)(2,1)}, bf16[4,136,360]{2,1,0:T(8,128)(2,1)}, u32[]{:S(2)}, u32[]{:S(2)}) collective-permute-start(bf16[4,136,360]{2,1,0:T(8,128)(2,1)} %copy-done.17), channel_id=1, source_target_pairs={{0,96},{1,97},{2,98},{3,99},{4,64},{5,65},{6,66},{7,67},{8,104},{9... | collective-permute-start | bytes 1175048 | tf_op jit(solution)/shard_map/ppermute | solution.py:287
  119.9 24.8 %collective-permute-start.6 = (bf16[4,136,360]{2,1,0:T(8,128)(2,1)}, bf16[4,136,360]{2,1,0:T(8,128)(2,1)}, u32[]{:S(2)}, u32[]{:S(2)}) collective-permute-start(bf16[4,136,360]{2,1,0:T(8,128)(2,1)} %copy-done.16), channel_id=1, source_target_pairs={{0,224},{1,225},{2,226},{3,227},{4,192},{5,193},{6,194},{7,195},{8... | collective-permute-start | bytes 1175048 | tf_op jit(solution)/shard_map/ppermute | solution.py:287
  145.6 27.7 %all-to-all-start.1 = ((bf16[16,136,360]{2,1,0:T(8,128)(2,1)}), bf16[16,136,360]{2,1,0:T(8,128)(2,1)S(1)}, u32[]{:S(2)}, u32[]{:S(2)}) async-start(bf16[16,136,360]{2,1,0:T(8,128)(2,1)} %copy-done.3), calls=%async_computation.1 | async-start | bytes 3342336 | tf_op jit(solution)/shard_map/all_to_all | solution.py:332
  151.9 6.6 %collective-permute-start.7 = (bf16[4,136,360]{2,1,0:T(8,128)(2,1)}, bf16[4,136,360]{2,1,0:T(8,128)(2,1)S(1)}, u32[]{:S(2)}, u32[]{:S(2)}) collective-permute-start(bf16[4,136,360]{2,1,0:T(8,128)(2,1)} %copy-done.15), channel_id=1, source_target_pairs={{0,32},{1,33},{2,34},{3,35},{4,0},{5,1},{6,2},{7,3},{8,40},{9,41},... | collective-permute-start | bytes 1175048 | tf_op jit(solution)/shard_map/ppermute | solution.py:287
  173.3 24.8 %copy-start.6 = (bf16[32,4,2880]{2,1,0:T(4,128)(2,1)S(1)}, bf16[32,4,2880]{2,1,0:T(4,128)(2,1)}, u32[]{:S(2)}) copy-start(bf16[32,4,2880]{2,1,0:T(4,128)(2,1)} %copy-done.5) | copy-start | bytes 2211844
  202.5 14.7 %all-to-all-start.3 = ((bf16[32,4,2880]{2,1,0:T(4,128)(2,1)}), bf16[32,4,2880]{2,1,0:T(4,128)(2,1)}, u32[]{:S(2)}, u32[]{:S(2)}) async-start(bf16[32,4,2880]{2,1,0:T(4,128)(2,1)} %copy-done.7), calls=%async_computation.3 | async-start | bytes 1507328 | tf_op jit(solution)/shard_map/all_to_all | solution.py:336
  213.1 28.3 %copy-start.19 = (f32[2,4,2880]{2,1,0:T(4,128)S(1)}, f32[2,4,2880]{2,1,0:T(4,128)}, u32[]{:S(2)}) copy-start(f32[2,4,2880]{2,1,0:T(4,128)} %copy-done.18) | copy-start | bytes 276484
  (12 other events, 12.7 us)

commit v3 on v2

v3 whole, which is shorter than its diff:
```python
import math

import jax
import jax.numpy as jnp
import numpy as np
from jax import lax
from jax.experimental import pallas as pl
from jax.experimental.pallas import tpu as pltpu
from jax.sharding import Mesh
from jax.sharding import PartitionSpec as P

D = 2880
QH = 32
KVH = 4
HD = 64
TOP = 4
NEG = -1e30
BF = jnp.bfloat16
F32 = jnp.float32
NT = (((1,), (1,)), ((), ()))
CACHE = ("zh", "core")
EXPERT = ("x", "zl", "y")
HOPS = 4
CORES = 2
ROWS = 136
PIECES = ((2, 0, 136), (0, 0, 136), (1, 0, 136), (3, 0, 136))


def params(mib):
    return pltpu.CompilerParams(vmem_limit_bytes=mib << 20)


def pack_kernel(place_ref, gate_ref, up_ref, down_ref, *refs):
    out_refs, block_ref, sems = refs[:-2], refs[-2], refs[-1]
    blocks, experts = block_ref.shape[0], block_ref.shape[1]
    depth = gate_ref.shape[0]
    half = depth // 2
    width = gate_ref.shape[2] // blocks
    for k in range(experts):
        gate = gate_ref[:, k, :]
        up = up_ref[:, k, :]
        down = down_ref[:, k, :]
        for c in range(blocks):
            cut = slice(c * width, (c + 1) * width)
            block_ref[c, k, 0:depth, :] = jnp.concatenate([gate[:, cut], up[:, cut]], axis=1)
            block_ref[c, k, depth : depth + half, :] = jnp.concatenate(
                [down[0:half, cut], down[half:depth, cut]], axis=1
            )
    copies = [
        pltpu.make_async_copy(
            block_ref.at[pl.ds(place_ref[i] * CORES, CORES), :, start : start + size], out_refs[i], sems.at[i]
        )
        for i, (_, start, size) in enumerate(PIECES)
    ]
    for copy in copies:
        copy.start()
    for copy in copies:
        copy.wait()


def pack(places, gate, up, down):
    depth, experts, width = gate.shape
    blocks = HOPS * CORES
    columns = 2 * width // blocks
    whole = whole_spec(gate.shape)
    outs = [jax.ShapeDtypeStruct((CORES, experts, size, columns), BF) for _, _, size in PIECES]
    grid_spec = pltpu.PrefetchScalarGridSpec(
        num_scalar_prefetch=1,
        grid=(1,),
        in_specs=[whole, whole, whole],
        out_specs=[pl.BlockSpec(memory_space=pltpu.HBM)] * len(outs),
        scratch_shapes=[
            pltpu.VMEM((blocks, experts, ROWS, columns), BF),
            pltpu.SemaphoreType.DMA((len(outs),)),
        ],
    )
    return pl.pallas_call(
        pack_kernel,
        grid_spec=grid_spec,
        out_shape=outs,
        compiler_params=params(24),
        name="pack",
    )(places, gate, up, down)


def join_kernel(place_ref, *refs):
    in_refs, out_ref, sems = refs[:-2], refs[-2], refs[-1]
    copies = [
        pltpu.make_async_copy(in_ref, out_ref.at[:, place_ref[i], :, start : start + size], sems.at[i])
        for i, (in_ref, (_, start, size)) in enumerate(zip(in_refs, PIECES))
    ]
    for copy in copies:
        copy.start()
    for copy in copies:
        copy.wait()


def join(places, pieces):
    _, experts, _, columns = pieces[0].shape
    grid_spec = pltpu.PrefetchScalarGridSpec(
        num_scalar_prefetch=1,
        grid=(1,),
        in_specs=[pl.BlockSpec(memory_space=pl.ANY)] * len(pieces),
        out_specs=pl.BlockSpec(memory_space=pl.ANY),
        scratch_shapes=[pltpu.SemaphoreType.DMA((len(pieces),))],
    )
    joined = pl.pallas_call(
        join_kernel,
        grid_spec=grid_spec,
        out_shape=jax.ShapeDtypeStruct((CORES, HOPS, experts, ROWS, columns), BF),
        compiler_params=params(8),
        name="join",
    )(places, *pieces)
    return joined.reshape(CORES * HOPS * experts, ROWS, columns)


def attend_kernel(length_ref, base_ref, query_ref, key_ref, value_ref, out_ref):
    row = pl.program_id(0)
    heads = query_ref.shape[1]
    positions = key_ref.shape[1]
    scores = lax.dot_general(query_ref[0], key_ref[0], NT, preferred_element_type=F32)
    scores = scores * (1.0 / math.sqrt(HD))
    position = base_ref[0] + lax.broadcasted_iota(jnp.int32, (heads, positions), 1)
    step = (lax.broadcasted_iota(jnp.int32, (heads, positions), 0) >= heads // 2).astype(jnp.int32)
    visible = position < length_ref[row] + 1 + step
    highest = jnp.max(jnp.where(visible, scores, NEG), axis=-1, keepdims=True)
    highest = highest.astype(BF).astype(F32)
    weights = jnp.where(visible, jnp.exp(scores - highest), 0.0)
    mass = jnp.sum(weights, axis=-1, keepdims=True)
    wide = jnp.dot(weights.astype(BF), value_ref[0], preferred_element_type=F32)
    group = heads // (2 * KVH)
    own = (lax.broadcasted_iota(jnp.int32, (heads, HD), 0) // group) % KVH
    accum = jnp.zeros((heads, HD), F32)
    for h in range(KVH):
        accum = accum + jnp.where(own == h, wide[:, h * HD : (h + 1) * HD], 0.0)
    lane = lax.broadcasted_iota(jnp.int32, (heads, HD), 1)
    extra = jnp.where(lane == 0, highest, jnp.where(lane == 1, mass, 0.0))
    result = jnp.concatenate([accum, extra], axis=1)
    count = out_ref.shape[0]
    per = heads // (2 * count)
    for c in range(count):
        out_ref[c, 0] = jnp.concatenate(
            [result[c * per : (c + 1) * per], result[heads // 2 + c * per : heads // 2 + (c + 1) * per]], axis=0
        )


def attend(lengths, base, query, keys, values, count):
    rows, heads, width = query.shape
    positions = keys.shape[1]
    grid_spec = pltpu.PrefetchScalarGridSpec(
        num_scalar_prefetch=2,
        grid=(rows,),
        in_specs=[
            pl.BlockSpec((1, heads, width), lambda r, *_: (r, 0, 0)),
            pl.BlockSpec((1, positions, width), lambda r, *_: (r, 0, 0)),
            pl.BlockSpec((1, positions, width), lambda r, *_: (r, 0, 0)),
        ],
        out_specs=pl.BlockSpec((count, 1, heads // count, 2 * HD), lambda r, *_: (0, r, 0, 0)),
    )
    return pl.pallas_call(
        attend_kernel,
        grid_spec=grid_spec,
        out_shape=jax.ShapeDtypeStruct((count, rows, heads // count, 2 * HD), F32),
        compiler_params=params(12),
        name="attend",
    )(lengths, base, query, keys, values)


def stack(weights_ref, first_ref, second_ref):
    sources = weights_ref.shape[0]
    width = second_ref.shape[1]
    depth = first_ref.shape[0] // sources
    half = depth // 2
    per = sources // (CORES * HOPS)
    for i in range(sources):
        core, x, y = i // (HOPS * per), i // per % HOPS, i % per
        at = ((x * CORES + core) * per + y) * depth
        block = weights_ref[i]
        first_ref[at : at + depth, :] = block[0:depth]
        second_ref[at : at + half, :] = block[depth : depth + half, 0:width]
        second_ref[at + half : at + depth, :] = block[depth : depth + half, width : 2 * width]


def expert_kernel(slots_ref, weights_ref, out_ref, first_ref, second_ref):
    width = second_ref.shape[1]
    stack(weights_ref, first_ref, second_ref)
    slots = slots_ref[...].reshape(out_ref.shape[0] * out_ref.shape[1], out_ref.shape[2])
    both = jnp.dot(slots, first_ref[...], preferred_element_type=F32)
    gate = both[:, 0:width]
    up = both[:, width : 2 * width]
    hidden = (gate * jax.nn.sigmoid(gate) * up).astype(BF)
    out = lax.dot_general(hidden, second_ref[...], NT, preferred_element_type=F32)
    out_ref[...] = out.astype(BF).reshape(out_ref.shape)


def whole_spec(shape):
    zeros = (0,) * len(shape)
    return pl.BlockSpec(shape, lambda i, *_: zeros)


def expert(slots, weights):
    width = weights.shape[2]
    return pl.pallas_call(
        expert_kernel,
        out_shape=jax.ShapeDtypeStruct(slots.shape, BF),
        scratch_shapes=[pltpu.VMEM((D, width), BF), pltpu.VMEM((D, width // 2), BF)],
        compiler_params=params(28),
        name="expert",
    )(slots, weights)


def owner_kernel(weights_ref, gate_ref, up_ref, down_ref, first_ref, second_ref):
    width = second_ref.shape[1]
    stack(weights_ref, first_ref, second_ref)
    row = lax.broadcasted_iota(jnp.int32, (width, 2 * width), 0)
    lane = lax.broadcasted_iota(jnp.int32, (width, 2 * width), 1)
    first = first_ref[...]
    pick = (row == lane).astype(BF)
    gate_ref[...] = lax.dot_general(pick, first, NT, preferred_element_type=F32).astype(BF)
    pick = (row + width == lane).astype(BF)
    up_ref[...] = lax.dot_general(pick, first, NT, preferred_element_type=F32).astype(BF)
    row = lax.broadcasted_iota(jnp.int32, (width, width), 0)
    lane = lax.broadcasted_iota(jnp.int32, (width, width), 1)
    pick = (row == lane).astype(BF)
    down_ref[...] = lax.dot_general(pick, second_ref[...], NT, preferred_element_type=F32).astype(BF)


def owner(weights):
    width = weights.shape[2]
    shape = jax.ShapeDtypeStruct((width // 2, D), BF)
    return pl.pallas_call(
        owner_kernel,
        out_shape=(shape, shape, shape),
        scratch_shapes=[pltpu.VMEM((D, width), BF), pltpu.VMEM((D, width // 2), BF)],
        compiler_params=params(28),
        name="owner",
    )(weights)


def along_z(hi):
    shape = (4, 2, 4, 2, 4)
    pairs = []
    for zh, core, x, zl, y in np.ndindex(shape):
        target = ((zh + hi) % 4, zl, x, core, y)
        pairs.append((int(np.ravel_multi_index((zh, core, x, zl, y), shape)), int(np.ravel_multi_index(target, shape))))
    return pairs


def shards(
    queries,
    k_cache,
    v_cache,
    lengths,
    w_out,
    norm_gain,
    w_gate,
    w_up,
    w_down,
    expert_ids,
    gate_weights,
):
    cache_count = lax.axis_size(CACHE)
    cache_place = lax.axis_index(CACHE)
    step_count = queries.shape[0]
    row_count, positions = k_cache.shape[0], k_cache.shape[1]
    group_size = QH // KVH

    zh = lax.axis_index("zh")
    packed = pack(
        jnp.stack([(zh + hi) % HOPS for hi, _, _ in PIECES]).astype(jnp.int32),
        jnp.transpose(w_gate, (1, 0, 2)),
        jnp.transpose(w_up, (1, 0, 2)),
        jnp.transpose(w_down, (2, 0, 1)),
    )
    packed, queries = lax.optimization_barrier((packed, queries))
    moved = [lax.ppermute(block, CACHE + EXPERT, along_z(piece[0])) for block, piece in zip(packed, PIECES)]

    query = queries.reshape(step_count, row_count, KVH, group_size, HD)
    query = jnp.transpose(query, (1, 0, 2, 3, 4))
    eye = jnp.eye(KVH, dtype=BF)
    query = query[:, :, :, :, None, :] * eye[None, None, :, None, :, None]
    query = query.reshape(row_count, step_count * QH, KVH * HD)
    base = (cache_place * positions).astype(jnp.int32).reshape(1)
    part = attend(lengths, base, query, k_cache, v_cache, cache_count)
    parts = lax.all_to_all(part, CACHE, split_axis=0, concat_axis=0, tiled=True)
    parts, moved[:2] = lax.optimization_barrier((parts, moved[:2]))

    own_heads = QH // cache_count
    parts = parts.reshape(cache_count, row_count, step_count, own_heads, 2 * HD)
    part_high = parts[..., HD : HD + 1]
    part_mass = parts[..., HD + 1 : HD + 2]
    factor = jnp.exp(part_high - jnp.max(part_high, axis=0))
    own_out = jnp.sum(parts[..., 0:HD] * factor, axis=0) / jnp.sum(part_mass * factor, axis=0)
    own_rows = jnp.transpose(own_out.astype(BF), (1, 0, 2, 3)).reshape(step_count * row_count, own_heads * HD)
    projected = jnp.dot(own_rows, w_out, preferred_element_type=F32).astype(BF)
    projected = jnp.broadcast_to(projected[None], (cache_count, *projected.shape))
    projected = lax.all_to_all(projected, CACHE, split_axis=0, concat_axis=0, tiled=True)
    projected, moved[2:4] = lax.optimization_barrier((projected, moved[2:4]))
    attention = jnp.sum(projected.astype(F32), axis=0)
    scale = lax.rsqrt(jnp.mean(attention * attention, axis=-1, keepdims=True) + 1e-05)
    normed = (attention * scale * norm_gain).astype(BF).reshape(step_count, row_count, D)

    experts_total = w_gate.shape[0] * cache_count
    capacity = max(2, (row_count * TOP + experts_total - 1) // experts_total)
    expert_range = jnp.arange(experts_total, dtype=jnp.int32)
    onehot = (expert_ids[..., None] == expert_range).astype(F32)
    chosen = jnp.sum(onehot, axis=2)
    gate_map = jnp.sum(onehot * gate_weights[..., None], axis=2)
    earlier = jnp.tril(jnp.ones((row_count, row_count), F32), -1)
    ranks = jnp.einsum("rq,sqe->sre", earlier, chosen, precision=lax.Precision.HIGHEST)
    slot_table = (ranks[..., None] == jnp.arange(capacity, dtype=F32)).astype(F32) * chosen[..., None]
    outgoing = jnp.einsum("srec,srd->escd", slot_table.astype(BF), normed, preferred_element_type=F32)
    outgoing = outgoing.astype(BF).reshape(experts_total, step_count * capacity, D)
    slots = lax.all_to_all(outgoing, EXPERT, split_axis=0, concat_axis=0, tiled=True)

    turns = jnp.stack([(zh - hi) % HOPS for hi, _, _ in PIECES]).astype(jnp.int32)
    slots, moved = lax.optimization_barrier((slots, moved))
    arrived = lax.all_to_all(join(turns, moved), ("core", "x", "y"), split_axis=0, concat_axis=0, tiled=True)
    partial_out = expert(slots, arrived)
    returned = lax.all_to_all(partial_out, EXPERT, split_axis=0, concat_axis=0, tiled=True)
    arrived, partial_out = lax.optimization_barrier((arrived, partial_out))
    gate_owner, up_owner, down_owner = owner(arrived)

    returned = returned.reshape(experts_total, step_count, capacity, D)
    combined = jnp.einsum(
        "srec,escd->srd",
        slot_table * gate_map[..., None],
        returned.astype(F32),
        precision=lax.Precision.HIGHEST,
    )
    shares = lax.all_gather(combined.astype(BF), CACHE, axis=0)
    total = jnp.sum(shares.astype(F32), axis=0) + attention.reshape(step_count, row_count, D)
    mixed = total.astype(BF)
    return (mixed, gate_owner.T[None], up_owner.T[None], down_owner[None])


def solution(mesh):
    return jax.shard_map(
        shards,
        mesh=Mesh(mesh.devices.reshape(4, 2, 4, 2, 4), CACHE + EXPERT),
        in_specs=(
            P(None, EXPERT, None),
            P(EXPERT, CACHE, None),
            P(EXPERT, CACHE, None),
            P(EXPERT),
            P(CACHE, None),
            P(),
            P(CACHE, EXPERT, None),
            P(CACHE, EXPERT, None),
            P(CACHE, None, EXPERT),
            P(None, EXPERT, None),
            P(None, EXPERT, None),
        ),
        out_specs=(
            P(None, EXPERT, None),
            P(EXPERT, None, CACHE),
            P(EXPERT, None, CACHE),
            P(EXPERT, CACHE, None),
        ),
        check_vma=False,
    )
```

time: 243 us -> 221 us (0.909)
  blocking collectives: 110 us -> 85.4 us
  waiting for transfers between devices: 38.3 us -> 59.1 us
  starting transfers between devices: 43.1 us -> 29.4 us
  Pallas kernels: 25.5 us -> 22.3 us
    all_gather x2 -> x0, blocking collectives: 63.2 us -> none  [the longest x1 47.8 us: shards(): parts = lax.all_gather(part, CACHE, axis=0)]
    all_to_all x1 -> x2, blocking collectives: 24.8 us -> 66.3 us  [the longest x1 48.9 us: shards(): lax.all_to_all(join(turns, moved), ('core', 'x', 'y'), split_axis=0, conc...]
    all_to_all x2, waiting for transfers between devices: 10.7 us -> 32.2 us  [the longest x1 28.5 us: shards(): parts = lax.all_to_all(part, CACHE, split_axis=0, concat_axis=0, tiled=True)]
    ppermute x8 -> x4, starting transfers between devices: 22.3 us -> 13.9 us  [shards(): lax.ppermute(block, CACHE + EXPERT, along_z(piece[0]))]
    all_to_all x2, starting transfers between devices: 16 us -> 11.5 us  [the longest x1 7.98 us: shards(): lax.all_to_all(projected, CACHE, split_axis=0, concat_axis=0, tiled=True)]
    ppermute x8 -> x4, waiting for transfers between devices: 23.5 us -> 19.9 us  [shards(): lax.ppermute(block, CACHE + EXPERT, along_z(piece[0]))]
    all_gather x1, blocking collectives: 22.2 us -> 19.1 us  [shards(): shares = lax.all_gather(combined.astype(BF), CACHE, axis=0)]
    all_to_all x1, waiting for transfers between devices: 4.18 us -> 7.1 us  [shards(): lax.all_to_all(partial_out, EXPERT, split_axis=0, concat_axis=0, tiled=True)]
  transfers between devices with their start and end apart: 11 -> 7, of which waited for: 4 -> 5; matrix products, arithmetic and copies ran while one was open for 1% -> 3% of each run, Pallas kernels for 5% -> 4%
where the time goes in v3:
time: 221 us; the launch traced here: 220 us
  blocking collectives  85.4 us (39%)
  waiting for transfers between devices  59.1 us (27%)
  starting transfers between devices  29.4 us (13%)
  Pallas kernels  22.3 us (10%)
  local copies, waits for them, and re-layouts  18 us (8%)
  other arithmetic  3.38 us (2%)
    all_to_all x1, blocking collectives, shards(): lax.all_to_all(join(turns, moved), ('core', 'x', 'y'), split_axis=0, conc...  48.9 us
    all_to_all x1, waiting for transfers between devices, shards(): parts = lax.all_to_all(part, CACHE, split_axis=0, concat_axis=0, tiled=True)  28.5 us
    ppermute x4, waiting for transfers between devices, shards(): lax.ppermute(block, CACHE + EXPERT, along_z(piece[0]))  19.9 us
    all_gather x1, blocking collectives, shards(): shares = lax.all_gather(combined.astype(BF), CACHE, axis=0)  19.1 us
    all_to_all x1, blocking collectives, shards(): lax.all_to_all(outgoing, EXPERT, split_axis=0, concat_axis=0, tiled=True)  17.4 us
    unnamed x34, local copies, waits for them, and re-layouts  14.3 us
    ppermute x4, starting transfers between devices, shards(): lax.ppermute(block, CACHE + EXPERT, along_z(piece[0]))  13.9 us
    pallas_call x1, Pallas kernels, pack(): pl.pallas_call(pack_kernel, grid_spec=grid_spec, out_shape=outs, compiler...  9.88 us
  transfers between devices with their start and end apart: 7, of which 5 were waited for; matrix products, arithmetic and copies ran while one was open for 3% of the time, Pallas kernels for 4%

profile of v3, /device:TPU:1, one launch (start us, length us, event | category | flops | bytes accessed | tf_op | source)
XLA Modules:
  0.0 220.1 jit_solution(14684736045645927613)
XLA Ops:
  0.8 1.3 copy-done.5
  2.1 1.2 copy-done.6
  4.6 9.9 %pack.1 = (bf16[2,4,136,360]{3,2,1,0:T(8,128)(2,1)}, bf16[2,4,136,360]{3,2,1,0:T(8,128)(2,1)}, bf16[2,4,136,360]{3,2,1,0:T(8,128)(2,1)S(1)}, bf16[2,4,136,360]{3,2,1,0:T(8,128)(2,1)S(1)}) custom-call(s32[4]{0:T(128)S(1)} %get-tuple-element.59.place_ref, bf16[90,4,1440]{2,1,0:T(4,128)(2,1)S(1)} %bitcast.54, bf16[90,4,1440]{2,1,0:T(4,128)(2,1)S(1)} %bitcast.55, ...), custom_call_target="tpu_custom_call" | custom-call | tf_op jit(solution)/shard_map/pack/pallas_call | solution.py:77
  16.3 7.9 %collective-permute-start = (bf16[2,4,136,360]{3,2,1,0:T(8,128)(2,1)}, bf16[2,4,136,360]{3,2,1,0:T(8,128)(2,1)S(1)}, u32[]{:S(2)}, u32[]{:S(2)}) collective-permute-start(bf16[2,4,136,360]{3,2,1,0:T(8,128)(2,1)} %get-tuple-element.33), channel_id=1, source_target_pairs={{0,128},{1,129},{2,130},{3,131},{4,160},{5,161},{6,162},{7,163},{8... | collective-permute-start | bytes 2350088 | tf_op jit(solution)/shard_map/ppermute | solution.py:276
  24.2 2.3 %collective-permute-start.1 = (bf16[2,4,136,360]{3,2,1,0:T(8,128)(2,1)}, bf16[2,4,136,360]{3,2,1,0:T(8,128)(2,1)S(1)}, u32[]{:S(2)}, u32[]{:S(2)}) collective-permute-start(bf16[2,4,136,360]{3,2,1,0:T(8,128)(2,1)} %get-tuple-element.34), channel_id=1, source_target_pairs={{0,0},{1,1},{2,2},{3,3},{4,32},{5,33},{6,34},{7,35},{8,8},{9,9},{1... | collective-permute-start | bytes 2350088 | tf_op jit(solution)/shard_map/ppermute | solution.py:276
  28.6 1.6 copy-done.3
  30.2 1.6 copy-done.4
  31.8 4.1 %attend.1 = f32[8,4,8,128]{3,2,1,0:T(8,128)} custom-call(s32[4]{0:T(128)S(1)} %copy-done.8, s32[1]{0:T(128)} %bitcast.2.base_ref, bf16[4,64,256]{2,1,0:T(8,128)(2,1)S(1)} %broadcast_multiply_fusion.query_ref, bf16[4,1024,256]{2,1,0:T(8,128)(2,1)S(1)} %copy-done.3, bf16[4,1024,256]{2,1,0:T(8,128)(2,1)S(1)} %copy-done.4), custom_call_target="tpu_custom_call" | custom-call | tf_op jit(solution)/shard_map/attend/pallas_call | solution.py:160
  35.9 3.5 %all-to-all-start = ((f32[8,4,8,128]{3,2,1,0:T(8,128)}), f32[8,4,8,128]{3,2,1,0:T(8,128)S(1)}, u32[]{:S(2)}, u32[]{:S(2)}) async-start(f32[8,4,8,128]{3,2,1,0:T(8,128)} %attend.1), calls=%async_computation | async-start | bytes 262144 | tf_op jit(solution)/shard_map/all_to_all | solution.py:285
  39.5 3.4 %collective-permute-start.2 = (bf16[2,4,136,360]{3,2,1,0:T(8,128)(2,1)}, bf16[2,4,136,360]{3,2,1,0:T(8,128)(2,1)}, u32[]{:S(2)}, u32[]{:S(2)}) collective-permute-start(bf16[2,4,136,360]{3,2,1,0:T(8,128)(2,1)} %copy-done.10), channel_id=1, source_target_pairs={{0,64},{1,65},{2,66},{3,67},{4,96},{5,97},{6,98},{7,99},{8,72},{9,... | collective-permute-start | bytes 2350088 | tf_op jit(solution)/shard_map/ppermute | solution.py:276
  43.2 28.5 %all-to-all-done = f32[8,4,8,128]{3,2,1,0:T(8,128)S(1)} async-done(((f32[8,4,8,128]{3,2,1,0:T(8,128)}), f32[8,4,8,128]{3,2,1,0:T(8,128)S(1)}, u32[]{:S(2)}, u32[]{:S(2)}) %all-to-all-start) | async-done | bytes 131104 | tf_op jit(solution)/shard_map/all_to_all | solution.py:285
  75.9 8.0 %all-to-all-start.1 = ((bf16[8,8,2880]{2,1,0:T(8,128)(2,1)}), bf16[8,8,2880]{2,1,0:T(8,128)(2,1)S(1)}, u32[]{:S(2)}, u32[]{:S(2)}) async-start(bf16[8,8,2880]{2,1,0:T(8,128)(2,1)} %broadcast_in_dim.8), calls=%async_computation.1 | async-start | bytes 753664 | tf_op jit(solution)/shard_map/all_to_all | solution.py:297
  84.2 18.9 %collective-permute-done.2.refs_2_ = bf16[2,4,136,360]{3,2,1,0:T(8,128)(2,1)} collective-permute-done((bf16[2,4,136,360]{3,2,1,0:T(8,128)(2,1)}, bf16[2,4,136,360]{3,2,1,0:T(8,128)(2,1)}, u32[]{:S(2)}, u32[]{:S(2)}) %collective-permute-start.2) | collective-permute-done | bytes 783392 | tf_op jit(solution)/shard_map/ppermute | solution.py:276
  104.0 3.6 %all-to-all-done.1 = bf16[8,8,2880]{2,1,0:T(8,128)(2,1)S(1)} async-done(((bf16[8,8,2880]{2,1,0:T(8,128)(2,1)}), bf16[8,8,2880]{2,1,0:T(8,128)(2,1)S(1)}, u32[]{:S(2)}, u32[]{:S(2)}) %all-to-all-start.1) | async-done | bytes 368672 | tf_op jit(solution)/shard_map/all_to_all | solution.py:297
  110.3 17.4 %all_to_all.25.slots_ref = bf16[32,4,2880]{2,1,0:T(4,128)(2,1)S(1)} all-to-all(bf16[32,4,2880]{2,1,0:T(4,128)(2,1)S(1)} %copy.40), channel_id=1, replica_groups=mesh['zh'=4,'core'=2,'x'=4,'zl'=2,'y'=4] {'x','zl','y'}, dimensions={0} | all-to-all | bytes 1474560 | tf_op jit(solution)/shard_map/all_to_all | solution.py:314
  127.7 2.2 join.1
  129.9 48.9 %all_to_all.26.weights_ref = bf16[32,136,360]{2,1,0:T(8,128)(2,1)S(1)} all-to-all(bf16[32,136,360]{2,1,0:T(8,128)(2,1)S(1)} %bitcast.53), channel_id=1, replica_groups=mesh['zh'=4,'core'=2,'x'=4,'zl'=2,'y'=4] {'core','x','y'}, dimensions={0} | all-to-all | bytes 6266880 | tf_op jit(solution)/shard_map/all_to_all | solution.py:318
  178.8 2.5 %expert.1 = bf16[32,4,2880]{2,1,0:T(4,128)(2,1)} custom-call(bf16[32,4,2880]{2,1,0:T(4,128)(2,1)S(1)} %all_to_all.25.slots_ref, bf16[32,136,360]{2,1,0:T(8,128)(2,1)S(1)} %all_to_all.26.weights_ref), custom_call_target="tpu_custom_call" | custom-call | tf_op jit(solution)/shard_map/expert/pallas_call | solution.py:203
  181.3 1.7 copy-done.1
  183.0 3.9 %all-to-all-start.4 = ((bf16[32,4,2880]{2,1,0:T(4,128)(2,1)}), bf16[32,4,2880]{2,1,0:T(4,128)(2,1)S(1)}, u32[]{:S(2)}, u32[]{:S(2)}) async-start(bf16[32,4,2880]{2,1,0:T(4,128)(2,1)} %expert.1), calls=%async_computation.4 | async-start | bytes 1507328 | tf_op jit(solution)/shard_map/all_to_all | solution.py:320
  186.9 1.9 copy-done.2
  188.9 3.6 %owner.1 = (bf16[180,2880]{1,0:T(8,128)(2,1)}, bf16[180,2880]{1,0:T(8,128)(2,1)}, bf16[180,2880]{1,0:T(8,128)(2,1)}) custom-call(bf16[32,136,360]{2,1,0:T(8,128)(2,1)S(1)} %copy-done.2), custom_call_target="tpu_custom_call" | custom-call | tf_op jit(solution)/shard_map/owner/pallas_call | solution.py:231
  192.5 7.1 %all-to-all-done.4 = bf16[32,4,2880]{2,1,0:T(4,128)(2,1)S(1)} async-done(((bf16[32,4,2880]{2,1,0:T(4,128)(2,1)}), bf16[32,4,2880]{2,1,0:T(4,128)(2,1)S(1)}, u32[]{:S(2)}, u32[]{:S(2)}) %all-to-all-start.4) | async-done | bytes 737312 | tf_op jit(solution)/shard_map/all_to_all | solution.py:320
  200.2 19.1 %all-gather = bf16[16,4,2880]{2,1,0:T(4,128)(2,1)S(1)} all-gather(bf16[2,4,2880]{2,1,0:T(4,128)(2,1)S(1)} %fusion), channel_id=2, replica_groups=mesh['zh'=4,'core'=2,'x'=4,'zl'=2,'y'=4] {'zh','core'}, dimensions={0}, use_global_device_ids=true | all-gather | bytes 414720 | tf_op jit(solution)/shard_map/all_gather | solution.py:331
  (64 shorter events, 14.8 us)
Async XLA Ops:
  0.6 73.9 %copy-start = (bf16[256,2880]{0,1:T(8,128)(2,1)S(1)}, bf16[256,2880]{0,1:T(8,128)(2,1)}, u32[]{:S(2)}) copy-start(bf16[256,2880]{0,1:T(8,128)(2,1)} %param.15) | copy-start | bytes 4423684
  0.8 1.3 copy-start.5
  2.1 1.2 copy-start.6
  3.4 1.2 copy-start.7
  4.6 22.7 %copy-start.12 = (bf16[2,4,2048]{2,1,0:T(4,128)(2,1)S(1)}, bf16[2,4,2048]{2,1,0:T(4,128)(2,1)}, u32[]{:S(2)}) copy-start(bf16[2,4,2048]{2,1,0:T(4,128)(2,1)} %param.11) | copy-start | bytes 98308
  4.6 24.0 %copy-start.8 = (s32[4]{0:T(128)S(1)}, s32[4]{0:T(128)}, u32[]{:S(2)}) copy-start(s32[4]{0:T(128)} %length_ref.1) | copy-start | bytes 52
  14.5 0.9 copy-start.9
  15.4 0.9 copy-start.10
  16.3 55.4 %collective-permute-start = (bf16[2,4,136,360]{3,2,1,0:T(8,128)(2,1)}, bf16[2,4,136,360]{3,2,1,0:T(8,128)(2,1)S(1)}, u32[]{:S(2)}, u32[]{:S(2)}) collective-permute-start(bf16[2,4,136,360]{3,2,1,0:T(8,128)(2,1)} %get-tuple-element.33), channel_id=1, source_target_pairs={{0,128},{1,129},{2,130},{3,131},{4,160},{5,161},{6,162},{7,163},{8... | collective-permute-start | bytes 2350088 | tf_op jit(solution)/shard_map/ppermute | solution.py:276
  24.2 47.6 %collective-permute-start.1 = (bf16[2,4,136,360]{3,2,1,0:T(8,128)(2,1)}, bf16[2,4,136,360]{3,2,1,0:T(8,128)(2,1)S(1)}, u32[]{:S(2)}, u32[]{:S(2)}) collective-permute-start(bf16[2,4,136,360]{3,2,1,0:T(8,128)(2,1)} %get-tuple-element.34), channel_id=1, source_target_pairs={{0,0},{1,1},{2,2},{3,3},{4,32},{5,33},{6,34},{7,35},{8,8},{9,9},{1... | collective-permute-start | bytes 2350088 | tf_op jit(solution)/shard_map/ppermute | solution.py:276
  28.6 1.6 copy-start.3
  30.2 1.6 copy-start.4
  35.9 35.8 %all-to-all-start = ((f32[8,4,8,128]{3,2,1,0:T(8,128)}), f32[8,4,8,128]{3,2,1,0:T(8,128)S(1)}, u32[]{:S(2)}, u32[]{:S(2)}) async-start(f32[8,4,8,128]{3,2,1,0:T(8,128)} %attend.1), calls=%async_computation | async-start | bytes 262144 | tf_op jit(solution)/shard_map/all_to_all | solution.py:285
  39.5 63.6 %collective-permute-start.2 = (bf16[2,4,136,360]{3,2,1,0:T(8,128)(2,1)}, bf16[2,4,136,360]{3,2,1,0:T(8,128)(2,1)}, u32[]{:S(2)}, u32[]{:S(2)}) collective-permute-start(bf16[2,4,136,360]{3,2,1,0:T(8,128)(2,1)} %copy-done.10), channel_id=1, source_target_pairs={{0,64},{1,65},{2,66},{3,67},{4,96},{5,97},{6,98},{7,99},{8,72},{9,... | collective-permute-start | bytes 2350088 | tf_op jit(solution)/shard_map/ppermute | solution.py:276
  42.9 61.1 %collective-permute-start.3 = (bf16[2,4,136,360]{3,2,1,0:T(8,128)(2,1)}, bf16[2,4,136,360]{3,2,1,0:T(8,128)(2,1)}, u32[]{:S(2)}, u32[]{:S(2)}) collective-permute-start(bf16[2,4,136,360]{3,2,1,0:T(8,128)(2,1)} %copy-done.9), channel_id=1, source_target_pairs={{0,192},{1,193},{2,194},{3,195},{4,224},{5,225},{6,226},{7,227},{8... | collective-permute-start | bytes 2350088 | tf_op jit(solution)/shard_map/ppermute | solution.py:276
  74.2 9.6 %copy-start.14 = (f32[2,4,4]{2,1,0:T(4,128)S(1)}, f32[2,4,4]{2,1,0:T(4,128)}, u32[]{:S(2)}) copy-start(f32[2,4,4]{2,1,0:T(4,128)} %param.21) | copy-start | bytes 388
  74.2 9.6 %copy-start.15 = (s32[2,4,4]{2,1,0:T(4,128)S(1)}, s32[2,4,4]{2,1,0:T(4,128)}, u32[]{:S(2)}) copy-start(s32[2,4,4]{2,1,0:T(4,128)} %param.20) | copy-start | bytes 388
  74.6 34.9 %copy-start.13 = (f32[2880]{0:T(1024)S(1)}, f32[2880]{0:T(1024)}, u32[]{:S(2)}) copy-start(f32[2880]{0:T(1024)} %param.16) | copy-start | bytes 34564
  75.9 31.8 %all-to-all-start.1 = ((bf16[8,8,2880]{2,1,0:T(8,128)(2,1)}), bf16[8,8,2880]{2,1,0:T(8,128)(2,1)S(1)}, u32[]{:S(2)}, u32[]{:S(2)}) async-start(bf16[8,8,2880]{2,1,0:T(8,128)(2,1)} %broadcast_in_dim.8), calls=%async_computation.1 | async-start | bytes 753664 | tf_op jit(solution)/shard_map/all_to_all | solution.py:297
  107.7 0.6 copy-start.11
  181.3 1.7 copy-start.1
  183.0 16.6 %all-to-all-start.4 = ((bf16[32,4,2880]{2,1,0:T(4,128)(2,1)}), bf16[32,4,2880]{2,1,0:T(4,128)(2,1)S(1)}, u32[]{:S(2)}, u32[]{:S(2)}) async-start(bf16[32,4,2880]{2,1,0:T(4,128)(2,1)} %expert.1), calls=%async_computation.4 | async-start | bytes 1507328 | tf_op jit(solution)/shard_map/all_to_all | solution.py:320
  186.9 1.9 copy-start.2

commit v4 on v3

--- a/solution.py
+++ b/solution.py
@@ -314,8 +314,8 @@
     slots = lax.all_to_all(outgoing, EXPERT, split_axis=0, concat_axis=0, tiled=True)
 
     turns = jnp.stack([(zh - hi) % HOPS for hi, _, _ in PIECES]).astype(jnp.int32)
-    slots, moved = lax.optimization_barrier((slots, moved))
-    arrived = lax.all_to_all(join(turns, moved), ("core", "x", "y"), split_axis=0, concat_axis=0, tiled=True)
+    joined, slots = lax.optimization_barrier((join(turns, moved), slots))
+    arrived = lax.all_to_all(joined, ("core", "x", "y"), split_axis=0, concat_axis=0, tiled=True)
     partial_out = expert(slots, arrived)
     returned = lax.all_to_all(partial_out, EXPERT, split_axis=0, concat_axis=0, tiled=True)
     arrived, partial_out = lax.optimization_barrier((arrived, partial_out))

time: 221 us -> 218 us (0.986)
  blocking collectives: 85.4 us -> 68.2 us
  starting transfers between devices: 29.4 us -> 40.9 us
    all_to_all x2 -> x1, blocking collectives: 66.3 us -> 49.1 us  [shards(): lax.all_to_all(joined, ('core', 'x', 'y'), split_axis=0, concat_axis=0, t...]
    all_to_all x0 -> x1, waiting for transfers between devices: none -> 7.34 us  [shards(): lax.all_to_all(outgoing, EXPERT, split_axis=0, concat_axis=0, tiled=True)]
    all_to_all x1, waiting for transfers between devices: 28.5 us -> 22.3 us  [shards(): parts = lax.all_to_all(part, CACHE, split_axis=0, concat_axis=0, tiled=True)]
    all_to_all x0 -> x1, starting transfers between devices: none -> 6.2 us  [shards(): lax.all_to_all(outgoing, EXPERT, split_axis=0, concat_axis=0, tiled=True)]
    all_to_all x1, starting transfers between devices: 3.55 us -> 9.68 us  [shards(): parts = lax.all_to_all(part, CACHE, split_axis=0, concat_axis=0, tiled=True)]
    unnamed x34 -> x32, local copies, waits for them, and re-layouts: 14.3 us -> 14.4 us
  transfers between devices with their start and end apart: 7 -> 8, of which waited for: 5 -> 6; matrix products, arithmetic and copies ran while one was open for 3% -> 3% of each run, Pallas kernels for 4% -> 5%
where the time goes in v4:
time: 218 us; the launch traced here: 217 us
  blocking collectives  68.2 us (31%)
  waiting for transfers between devices  61.1 us (28%)
  starting transfers between devices  40.9 us (19%)
  Pallas kernels  22.5 us (10%)
  local copies, waits for them, and re-layouts  18.1 us (8%)
  other arithmetic  3.38 us (2%)
    all_to_all x1, blocking collectives, shards(): lax.all_to_all(joined, ('core', 'x', 'y'), split_axis=0, concat_axis=0, t...  49.1 us
    all_to_all x1, waiting for transfers between devices, shards(): parts = lax.all_to_all(part, CACHE, split_axis=0, concat_axis=0, tiled=True)  22.3 us
    ppermute x4, waiting for transfers between devices, shards(): lax.ppermute(block, CACHE + EXPERT, along_z(piece[0]))  20.7 us
    all_gather x1, blocking collectives, shards(): shares = lax.all_gather(combined.astype(BF), CACHE, axis=0)  19.1 us
    unnamed x32, local copies, waits for them, and re-layouts  14.4 us
    ppermute x4, starting transfers between devices, shards(): lax.ppermute(block, CACHE + EXPERT, along_z(piece[0]))  13.2 us
    pallas_call x1, Pallas kernels, pack(): pl.pallas_call(pack_kernel, grid_spec=grid_spec, out_shape=outs, compiler...  9.87 us
    all_to_all x1, starting transfers between devices, shards(): parts = lax.all_to_all(part, CACHE, split_axis=0, concat_axis=0, tiled=True)  9.68 us
  transfers between devices with their start and end apart: 8, of which 6 were waited for; matrix products, arithmetic and copies ran while one was open for 3% of the time, Pallas kernels for 5%

profile of v4, /device:TPU:1, one launch (start us, length us, event | category | flops | bytes accessed | tf_op | source)
XLA Modules:
  0.0 216.8 jit_solution(3565557405634484730)
XLA Ops:
  4.6 9.9 %pack.1 = (bf16[2,4,136,360]{3,2,1,0:T(8,128)(2,1)}, bf16[2,4,136,360]{3,2,1,0:T(8,128)(2,1)}, bf16[2,4,136,360]{3,2,1,0:T(8,128)(2,1)S(1)}, bf16[2,4,136,360]{3,2,1,0:T(8,128)(2,1)S(1)}) custom-call(s32[4]{0:T(128)S(1)} %get-tuple-element.54.place_ref, bf16[90,4,1440]{2,1,0:T(4,128)(2,1)S(1)} %bitcast.54, bf16[90,4,1440]{2,1,0:T(4,128)(2,1)S(1)} %bitcast.55, ...), custom_call_target="tpu_custom_call" | custom-call | tf_op jit(solution)/shard_map/pack/pallas_call | solution.py:77
  15.4 7.9 %collective-permute-start = (bf16[2,4,136,360]{3,2,1,0:T(8,128)(2,1)}, bf16[2,4,136,360]{3,2,1,0:T(8,128)(2,1)S(1)}, u32[]{:S(2)}, u32[]{:S(2)}) collective-permute-start(bf16[2,4,136,360]{3,2,1,0:T(8,128)(2,1)} %get-tuple-element.30), channel_id=1, source_target_pairs={{0,128},{1,129},{2,130},{3,131},{4,160},{5,161},{6,162},{7,163},{8... | collective-permute-start | bytes 2350088 | tf_op jit(solution)/shard_map/ppermute | solution.py:276
  23.3 2.3 %collective-permute-start.1 = (bf16[2,4,136,360]{3,2,1,0:T(8,128)(2,1)}, bf16[2,4,136,360]{3,2,1,0:T(8,128)(2,1)}, u32[]{:S(2)}, u32[]{:S(2)}) collective-permute-start(bf16[2,4,136,360]{3,2,1,0:T(8,128)(2,1)} %get-tuple-element.31), channel_id=1, source_target_pairs={{0,0},{1,1},{2,2},{3,3},{4,32},{5,33},{6,34},{7,35},{8,8},{9,9},{1... | collective-permute-start | bytes 2350088 | tf_op jit(solution)/shard_map/ppermute | solution.py:276
  27.7 1.6 copy-done.4
  29.3 1.6 copy-done.5
  30.9 4.1 %attend.1 = f32[8,4,8,128]{3,2,1,0:T(8,128)} custom-call(s32[4]{0:T(128)S(1)} %copy-done.9, s32[1]{0:T(128)} %bitcast.6.base_ref, bf16[4,64,256]{2,1,0:T(8,128)(2,1)S(1)} %broadcast_multiply_fusion.query_ref, bf16[4,1024,256]{2,1,0:T(8,128)(2,1)S(1)} %copy-done.4, bf16[4,1024,256]{2,1,0:T(8,128)(2,1)S(1)} %copy-done.5), custom_call_target="tpu_custom_call" | custom-call | tf_op jit(solution)/shard_map/attend/pallas_call | solution.py:160
  35.0 9.7 %all-to-all-start = ((f32[8,4,8,128]{3,2,1,0:T(8,128)}), f32[8,4,8,128]{3,2,1,0:T(8,128)S(1)}, u32[]{:S(2)}, u32[]{:S(2)}) async-start(f32[8,4,8,128]{3,2,1,0:T(8,128)} %attend.1), calls=%async_computation | async-start | bytes 262144 | tf_op jit(solution)/shard_map/all_to_all | solution.py:285
  44.7 1.6 collective-permute-start.2
  47.7 22.3 %all-to-all-done = f32[8,4,8,128]{3,2,1,0:T(8,128)S(1)} async-done(((f32[8,4,8,128]{3,2,1,0:T(8,128)}), f32[8,4,8,128]{3,2,1,0:T(8,128)S(1)}, u32[]{:S(2)}, u32[]{:S(2)}) %all-to-all-start) | async-done | bytes 131104 | tf_op jit(solution)/shard_map/all_to_all | solution.py:285
  74.0 8.0 %all-to-all-start.1 = ((bf16[8,8,2880]{2,1,0:T(8,128)(2,1)}), bf16[8,8,2880]{2,1,0:T(8,128)(2,1)S(1)}, u32[]{:S(2)}, u32[]{:S(2)}) async-start(bf16[8,8,2880]{2,1,0:T(8,128)(2,1)} %broadcast_in_dim.8), calls=%async_computation.1 | async-start | bytes 753664 | tf_op jit(solution)/shard_map/all_to_all | solution.py:297
  82.3 19.9 %collective-permute-done.2.refs_2_ = bf16[2,4,136,360]{3,2,1,0:T(8,128)(2,1)} collective-permute-done((bf16[2,4,136,360]{3,2,1,0:T(8,128)(2,1)}, bf16[2,4,136,360]{3,2,1,0:T(8,128)(2,1)}, u32[]{:S(2)}, u32[]{:S(2)}) %collective-permute-start.2) | collective-permute-done | bytes 783392 | tf_op jit(solution)/shard_map/ppermute | solution.py:276
  103.0 3.7 %all-to-all-done.1 = bf16[8,8,2880]{2,1,0:T(8,128)(2,1)S(1)} async-done(((bf16[8,8,2880]{2,1,0:T(8,128)(2,1)}), bf16[8,8,2880]{2,1,0:T(8,128)(2,1)S(1)}, u32[]{:S(2)}, u32[]{:S(2)}) %all-to-all-start.1) | async-done | bytes 368672 | tf_op jit(solution)/shard_map/all_to_all | solution.py:297
  108.8 6.2 %all-to-all-start.2 = ((bf16[32,4,2880]{2,1,0:T(4,128)(2,1)}), bf16[32,4,2880]{2,1,0:T(4,128)(2,1)S(1)}, u32[]{:S(2)}, u32[]{:S(2)}) async-start(bf16[32,4,2880]{2,1,0:T(4,128)(2,1)} %copy.40), calls=%async_computation.2 | async-start | bytes 1507328 | tf_op jit(solution)/shard_map/all_to_all | solution.py:314
  115.0 2.3 %join.1 = bf16[2,4,4,136,360]{4,3,2,1,0:T(8,128)(2,1)S(1)} custom-call(s32[4]{0:T(128)S(1)} %get-tuple-element.53.place_ref, bf16[2,4,136,360]{3,2,1,0:T(8,128)(2,1)S(1)} %collective-permute-done.refs_0_, bf16[2,4,136,360]{3,2,1,0:T(8,128)(2,1)} %collective-permute-done.1.refs_1_, bf16[2,4,136,360]{3,2,1,0:T(8,128)(2,1)} %collective-permute-done.2.refs_2_, ...), custom_call_target="tpu_custom_call" | custom-call | tf_op jit(solution)/shard_map/join/pallas_call | solution.py:107
  117.3 1.7 copy-done.3
  119.0 7.3 %all-to-all-done.2.slots_ref = bf16[32,4,2880]{2,1,0:T(4,128)(2,1)S(1)} async-done(((bf16[32,4,2880]{2,1,0:T(4,128)(2,1)}), bf16[32,4,2880]{2,1,0:T(4,128)(2,1)S(1)}, u32[]{:S(2)}, u32[]{:S(2)}) %all-to-all-start.2) | async-done | bytes 737312 | tf_op jit(solution)/shard_map/all_to_all | solution.py:314
  126.4 49.1 %all_to_all.25.weights_ref = bf16[32,136,360]{2,1,0:T(8,128)(2,1)S(1)} all-to-all(bf16[32,136,360]{2,1,0:T(8,128)(2,1)} %bitcast.53), channel_id=1, replica_groups=mesh['zh'=4,'core'=2,'x'=4,'zl'=2,'y'=4] {'core','x','y'}, dimensions={0} | all-to-all | bytes 6266880 | tf_op jit(solution)/shard_map/all_to_all | solution.py:318
  175.5 2.5 %expert.1 = bf16[32,4,2880]{2,1,0:T(4,128)(2,1)} custom-call(bf16[32,4,2880]{2,1,0:T(4,128)(2,1)S(1)} %all-to-all-done.2.slots_ref, bf16[32,136,360]{2,1,0:T(8,128)(2,1)S(1)} %all_to_all.25.weights_ref), custom_call_target="tpu_custom_call" | custom-call | tf_op jit(solution)/shard_map/expert/pallas_call | solution.py:203
  178.0 1.7 copy-done.1
  179.7 3.9 %all-to-all-start.4 = ((bf16[32,4,2880]{2,1,0:T(4,128)(2,1)}), bf16[32,4,2880]{2,1,0:T(4,128)(2,1)S(1)}, u32[]{:S(2)}, u32[]{:S(2)}) async-start(bf16[32,4,2880]{2,1,0:T(4,128)(2,1)} %expert.1), calls=%async_computation.4 | async-start | bytes 1507328 | tf_op jit(solution)/shard_map/all_to_all | solution.py:320
  183.7 1.9 copy-done.2
  185.6 3.6 %owner.1 = (bf16[180,2880]{1,0:T(8,128)(2,1)}, bf16[180,2880]{1,0:T(8,128)(2,1)}, bf16[180,2880]{1,0:T(8,128)(2,1)}) custom-call(bf16[32,136,360]{2,1,0:T(8,128)(2,1)S(1)} %copy-done.2), custom_call_target="tpu_custom_call" | custom-call | tf_op jit(solution)/shard_map/owner/pallas_call | solution.py:231
  189.3 7.1 %all-to-all-done.4 = bf16[32,4,2880]{2,1,0:T(4,128)(2,1)S(1)} async-done(((bf16[32,4,2880]{2,1,0:T(4,128)(2,1)}), bf16[32,4,2880]{2,1,0:T(4,128)(2,1)S(1)}, u32[]{:S(2)}, u32[]{:S(2)}) %all-to-all-start.4) | async-done | bytes 737312 | tf_op jit(solution)/shard_map/all_to_all | solution.py:320
  196.9 19.1 %all-gather = bf16[16,4,2880]{2,1,0:T(4,128)(2,1)S(1)} all-gather(bf16[2,4,2880]{2,1,0:T(4,128)(2,1)S(1)} %fusion), channel_id=2, replica_groups=mesh['zh'=4,'core'=2,'x'=4,'zl'=2,'y'=4] {'zh','core'}, dimensions={0}, use_global_device_ids=true | all-gather | bytes 414720 | tf_op jit(solution)/shard_map/all_gather | solution.py:331
  (63 shorter events, 16.8 us)
Async XLA Ops:
  0.6 72.1 %copy-start = (bf16[256,2880]{0,1:T(8,128)(2,1)S(1)}, bf16[256,2880]{0,1:T(8,128)(2,1)}, u32[]{:S(2)}) copy-start(bf16[256,2880]{0,1:T(8,128)(2,1)} %param.15) | copy-start | bytes 4423684
  0.8 1.3 copy-start.6
  2.1 1.2 copy-start.7
  3.4 1.2 copy-start.8
  4.6 21.8 %copy-start.11 = (bf16[2,4,2048]{2,1,0:T(4,128)(2,1)S(1)}, bf16[2,4,2048]{2,1,0:T(4,128)(2,1)}, u32[]{:S(2)}) copy-start(bf16[2,4,2048]{2,1,0:T(4,128)(2,1)} %param.11) | copy-start | bytes 98308
  4.6 23.0 %copy-start.9 = (s32[4]{0:T(128)S(1)}, s32[4]{0:T(128)}, u32[]{:S(2)}) copy-start(s32[4]{0:T(128)} %length_ref.1) | copy-start | bytes 52
  14.5 0.9 copy-start.10
  15.4 54.5 %collective-permute-start = (bf16[2,4,136,360]{3,2,1,0:T(8,128)(2,1)}, bf16[2,4,136,360]{3,2,1,0:T(8,128)(2,1)S(1)}, u32[]{:S(2)}, u32[]{:S(2)}) collective-permute-start(bf16[2,4,136,360]{3,2,1,0:T(8,128)(2,1)} %get-tuple-element.30), channel_id=1, source_target_pairs={{0,128},{1,129},{2,130},{3,131},{4,160},{5,161},{6,162},{7,163},{8... | collective-permute-start | bytes 2350088 | tf_op jit(solution)/shard_map/ppermute | solution.py:276
  23.3 46.7 %collective-permute-start.1 = (bf16[2,4,136,360]{3,2,1,0:T(8,128)(2,1)}, bf16[2,4,136,360]{3,2,1,0:T(8,128)(2,1)}, u32[]{:S(2)}, u32[]{:S(2)}) collective-permute-start(bf16[2,4,136,360]{3,2,1,0:T(8,128)(2,1)} %get-tuple-element.31), channel_id=1, source_target_pairs={{0,0},{1,1},{2,2},{3,3},{4,32},{5,33},{6,34},{7,35},{8,8},{9,9},{1... | collective-permute-start | bytes 2350088 | tf_op jit(solution)/shard_map/ppermute | solution.py:276
  27.7 1.6 copy-start.4
  29.3 1.6 copy-start.5
  35.0 34.9 %all-to-all-start = ((f32[8,4,8,128]{3,2,1,0:T(8,128)}), f32[8,4,8,128]{3,2,1,0:T(8,128)S(1)}, u32[]{:S(2)}, u32[]{:S(2)}) async-start(f32[8,4,8,128]{3,2,1,0:T(8,128)} %attend.1), calls=%async_computation | async-start | bytes 262144 | tf_op jit(solution)/shard_map/all_to_all | solution.py:285
  44.7 57.5 %collective-permute-start.2 = (bf16[2,4,136,360]{3,2,1,0:T(8,128)(2,1)}, bf16[2,4,136,360]{3,2,1,0:T(8,128)(2,1)}, u32[]{:S(2)}, u32[]{:S(2)}) collective-permute-start(bf16[2,4,136,360]{3,2,1,0:T(8,128)(2,1)} %copy-done.10), channel_id=1, source_target_pairs={{0,64},{1,65},{2,66},{3,67},{4,96},{5,97},{6,98},{7,99},{8,72},{9,... | collective-permute-start | bytes 2350088 | tf_op jit(solution)/shard_map/ppermute | solution.py:276
  46.3 56.7 %collective-permute-start.3 = (bf16[2,4,136,360]{3,2,1,0:T(8,128)(2,1)S(1)}, bf16[2,4,136,360]{3,2,1,0:T(8,128)(2,1)}, u32[]{:S(2)}, u32[]{:S(2)}) collective-permute-start(bf16[2,4,136,360]{3,2,1,0:T(8,128)(2,1)S(1)} %get-tuple-element.36), channel_id=1, source_target_pairs={{0,192},{1,193},{2,194},{3,195},{4,224},{5,225},{6,226},{7,227},{8... | collective-permute-start | bytes 2350088 | tf_op jit(solution)/shard_map/ppermute | solution.py:276
  72.4 9.6 %copy-start.13 = (f32[2,4,4]{2,1,0:T(4,128)S(1)}, f32[2,4,4]{2,1,0:T(4,128)}, u32[]{:S(2)}) copy-start(f32[2,4,4]{2,1,0:T(4,128)} %param.21) | copy-start | bytes 388
  72.4 9.6 %copy-start.14 = (s32[2,4,4]{2,1,0:T(4,128)S(1)}, s32[2,4,4]{2,1,0:T(4,128)}, u32[]{:S(2)}) copy-start(s32[2,4,4]{2,1,0:T(4,128)} %param.20) | copy-start | bytes 388
  72.7 34.3 %copy-start.12 = (f32[2880]{0:T(1024)S(1)}, f32[2880]{0:T(1024)}, u32[]{:S(2)}) copy-start(f32[2880]{0:T(1024)} %param.16) | copy-start | bytes 34564
  74.0 32.7 %all-to-all-start.1 = ((bf16[8,8,2880]{2,1,0:T(8,128)(2,1)}), bf16[8,8,2880]{2,1,0:T(8,128)(2,1)S(1)}, u32[]{:S(2)}, u32[]{:S(2)}) async-start(bf16[8,8,2880]{2,1,0:T(8,128)(2,1)} %broadcast_in_dim.8), calls=%async_computation.1 | async-start | bytes 753664 | tf_op jit(solution)/shard_map/all_to_all | solution.py:297
  108.8 17.6 %all-to-all-start.2 = ((bf16[32,4,2880]{2,1,0:T(4,128)(2,1)}), bf16[32,4,2880]{2,1,0:T(4,128)(2,1)S(1)}, u32[]{:S(2)}, u32[]{:S(2)}) async-start(bf16[32,4,2880]{2,1,0:T(4,128)(2,1)} %copy.40), calls=%async_computation.2 | async-start | bytes 1507328 | tf_op jit(solution)/shard_map/all_to_all | solution.py:314
  117.3 1.7 copy-start.3
  178.0 1.7 copy-start.1
  179.7 16.6 %all-to-all-start.4 = ((bf16[32,4,2880]{2,1,0:T(4,128)(2,1)}), bf16[32,4,2880]{2,1,0:T(4,128)(2,1)S(1)}, u32[]{:S(2)}, u32[]{:S(2)}) async-start(bf16[32,4,2880]{2,1,0:T(4,128)(2,1)} %expert.1), calls=%async_computation.4 | async-start | bytes 1507328 | tf_op jit(solution)/shard_map/all_to_all | solution.py:320
  183.7 1.9 copy-start.2

commit v5 on v4

--- a/solution.py
+++ b/solution.py
@@ -23,7 +23,7 @@
 HOPS = 4
 CORES = 2
 ROWS = 136
-PIECES = ((2, 0, 136), (0, 0, 136), (1, 0, 136), (3, 0, 136))
+PIECES = ((1, 0, 136), (3, 0, 136), (2, 0, 136), (0, 0, 136))
 
 
 def params(mib):

time: 218 us -> 219 us (level)
  starting transfers between devices: 40.9 us -> 52.6 us
  waiting for transfers between devices: 61.1 us -> 54.6 us
  blocking collectives: 68.2 us -> 64.1 us
    all_to_all x1, starting transfers between devices: 7.98 us -> 19.6 us  [shards(): lax.all_to_all(projected, CACHE, split_axis=0, concat_axis=0, tiled=True)]
    ppermute x4, waiting for transfers between devices: 20.7 us -> 10.2 us  [shards(): lax.ppermute(block, CACHE + EXPERT, along_z(piece[0]))]
    all_to_all x1, waiting for transfers between devices: 3.73 us -> 9.03 us  [shards(): lax.all_to_all(projected, CACHE, split_axis=0, concat_axis=0, tiled=True)]
    all_gather x1, blocking collectives: 19.1 us -> 16.1 us  [shards(): shares = lax.all_gather(combined.astype(BF), CACHE, axis=0)]
    all_to_all x1, starting transfers between devices: 9.68 us -> 7.14 us  [shards(): parts = lax.all_to_all(part, CACHE, split_axis=0, concat_axis=0, tiled=True)]
    all_to_all x1, waiting for transfers between devices: 22.3 us -> 19.8 us  [shards(): parts = lax.all_to_all(part, CACHE, split_axis=0, concat_axis=0, tiled=True)]
where the time goes in v5:
time: 219 us; the launch traced here: 218 us
  blocking collectives  64.1 us (29%)
  waiting for transfers between devices  54.6 us (25%)
  starting transfers between devices  52.6 us (24%)
  Pallas kernels  22.5 us (10%)
  local copies, waits for them, and re-layouts  18.1 us (8%)
  other arithmetic  3.38 us (2%)
    all_to_all x1, blocking collectives, shards(): lax.all_to_all(joined, ('core', 'x', 'y'), split_axis=0, concat_axis=0, t...  48 us
    all_to_all x1, waiting for transfers between devices, shards(): parts = lax.all_to_all(part, CACHE, split_axis=0, concat_axis=0, tiled=True)  19.8 us
    all_to_all x1, starting transfers between devices, shards(): lax.all_to_all(projected, CACHE, split_axis=0, concat_axis=0, tiled=True)  19.6 us
    all_gather x1, blocking collectives, shards(): shares = lax.all_gather(combined.astype(BF), CACHE, axis=0)  16.1 us
    ppermute x4, starting transfers between devices, shards(): lax.ppermute(block, CACHE + EXPERT, along_z(piece[0]))  14.9 us
    unnamed x32, local copies, waits for them, and re-layouts  14.4 us
    ppermute x4, waiting for transfers between devices, shards(): lax.ppermute(block, CACHE + EXPERT, along_z(piece[0]))  10.2 us
    pallas_call x1, Pallas kernels, pack(): pl.pallas_call(pack_kernel, grid_spec=grid_spec, out_shape=outs, compiler...  9.87 us
  transfers between devices with their start and end apart: 8, of which 6 were waited for; matrix products, arithmetic and copies ran while one was open for 3% of the time, Pallas kernels for 5%

profile of v5, /device:TPU:1, one launch (start us, length us, event | category | flops | bytes accessed | tf_op | source)
XLA Modules:
  0.0 217.8 jit_solution(5356235284237694075)
XLA Ops:
  4.6 9.9 %pack.1 = (bf16[2,4,136,360]{3,2,1,0:T(8,128)(2,1)}, bf16[2,4,136,360]{3,2,1,0:T(8,128)(2,1)}, bf16[2,4,136,360]{3,2,1,0:T(8,128)(2,1)S(1)}, bf16[2,4,136,360]{3,2,1,0:T(8,128)(2,1)S(1)}) custom-call(s32[4]{0:T(128)S(1)} %get-tuple-element.54.place_ref, bf16[90,4,1440]{2,1,0:T(4,128)(2,1)S(1)} %bitcast.54, bf16[90,4,1440]{2,1,0:T(4,128)(2,1)S(1)} %bitcast.55, ...), custom_call_target="tpu_custom_call" | custom-call | tf_op jit(solution)/shard_map/pack/pallas_call | solution.py:77
  15.4 5.7 %collective-permute-start = (bf16[2,4,136,360]{3,2,1,0:T(8,128)(2,1)}, bf16[2,4,136,360]{3,2,1,0:T(8,128)(2,1)S(1)}, u32[]{:S(2)}, u32[]{:S(2)}) collective-permute-start(bf16[2,4,136,360]{3,2,1,0:T(8,128)(2,1)} %get-tuple-element.30), channel_id=1, source_target_pairs={{0,64},{1,65},{2,66},{3,67},{4,96},{5,97},{6,98},{7,99},{8,72},{9,... | collective-permute-start | bytes 2350088 | tf_op jit(solution)/shard_map/ppermute | solution.py:276
  24.5 1.6 copy-done.4
  26.0 1.6 copy-done.5
  27.6 4.1 %attend.1 = f32[8,4,8,128]{3,2,1,0:T(8,128)} custom-call(s32[4]{0:T(128)S(1)} %copy-done.9, s32[1]{0:T(128)} %bitcast.6.base_ref, bf16[4,64,256]{2,1,0:T(8,128)(2,1)S(1)} %broadcast_multiply_fusion.query_ref, bf16[4,1024,256]{2,1,0:T(8,128)(2,1)S(1)} %copy-done.4, bf16[4,1024,256]{2,1,0:T(8,128)(2,1)S(1)} %copy-done.5), custom_call_target="tpu_custom_call" | custom-call | tf_op jit(solution)/shard_map/attend/pallas_call | solution.py:160
  31.8 7.1 %all-to-all-start = ((f32[8,4,8,128]{3,2,1,0:T(8,128)}), f32[8,4,8,128]{3,2,1,0:T(8,128)S(1)}, u32[]{:S(2)}, u32[]{:S(2)}) async-start(f32[8,4,8,128]{3,2,1,0:T(8,128)} %attend.1), calls=%async_computation | async-start | bytes 262144 | tf_op jit(solution)/shard_map/all_to_all | solution.py:285
  38.9 5.7 %collective-permute-start.2 = (bf16[2,4,136,360]{3,2,1,0:T(8,128)(2,1)}, bf16[2,4,136,360]{3,2,1,0:T(8,128)(2,1)}, u32[]{:S(2)}, u32[]{:S(2)}) collective-permute-start(bf16[2,4,136,360]{3,2,1,0:T(8,128)(2,1)} %copy-done.10), channel_id=1, source_target_pairs={{0,128},{1,129},{2,130},{3,131},{4,160},{5,161},{6,162},{7,163},{8... | collective-permute-start | bytes 2350088 | tf_op jit(solution)/shard_map/ppermute | solution.py:276
  44.6 2.2 %collective-permute-start.3 = (bf16[2,4,136,360]{3,2,1,0:T(8,128)(2,1)S(1)}, bf16[2,4,136,360]{3,2,1,0:T(8,128)(2,1)}, u32[]{:S(2)}, u32[]{:S(2)}) collective-permute-start(bf16[2,4,136,360]{3,2,1,0:T(8,128)(2,1)S(1)} %get-tuple-element.36), channel_id=1, source_target_pairs={{0,0},{1,1},{2,2},{3,3},{4,32},{5,33},{6,34},{7,35},{8,8},{9,9},{1... | collective-permute-start | bytes 2350088 | tf_op jit(solution)/shard_map/ppermute | solution.py:276
  46.9 19.8 %all-to-all-done = f32[8,4,8,128]{3,2,1,0:T(8,128)S(1)} async-done(((f32[8,4,8,128]{3,2,1,0:T(8,128)}), f32[8,4,8,128]{3,2,1,0:T(8,128)S(1)}, u32[]{:S(2)}, u32[]{:S(2)}) %all-to-all-start) | async-done | bytes 131104 | tf_op jit(solution)/shard_map/all_to_all | solution.py:285
  70.8 19.6 %all-to-all-start.1 = ((bf16[8,8,2880]{2,1,0:T(8,128)(2,1)}), bf16[8,8,2880]{2,1,0:T(8,128)(2,1)S(1)}, u32[]{:S(2)}, u32[]{:S(2)}) async-start(bf16[8,8,2880]{2,1,0:T(8,128)(2,1)} %broadcast_in_dim.8), calls=%async_computation.1 | async-start | bytes 753664 | tf_op jit(solution)/shard_map/all_to_all | solution.py:297
  90.7 8.7 %collective-permute-done.2.refs_2_ = bf16[2,4,136,360]{3,2,1,0:T(8,128)(2,1)} collective-permute-done((bf16[2,4,136,360]{3,2,1,0:T(8,128)(2,1)}, bf16[2,4,136,360]{3,2,1,0:T(8,128)(2,1)}, u32[]{:S(2)}, u32[]{:S(2)}) %collective-permute-start.2) | collective-permute-done | bytes 783392 | tf_op jit(solution)/shard_map/ppermute | solution.py:276
  100.9 9.0 %all-to-all-done.1 = bf16[8,8,2880]{2,1,0:T(8,128)(2,1)S(1)} async-done(((bf16[8,8,2880]{2,1,0:T(8,128)(2,1)}), bf16[8,8,2880]{2,1,0:T(8,128)(2,1)S(1)}, u32[]{:S(2)}, u32[]{:S(2)}) %all-to-all-start.1) | async-done | bytes 368672 | tf_op jit(solution)/shard_map/all_to_all | solution.py:297
  111.9 7.0 %all-to-all-start.2 = ((bf16[32,4,2880]{2,1,0:T(4,128)(2,1)}), bf16[32,4,2880]{2,1,0:T(4,128)(2,1)S(1)}, u32[]{:S(2)}, u32[]{:S(2)}) async-start(bf16[32,4,2880]{2,1,0:T(4,128)(2,1)} %copy.40), calls=%async_computation.2 | async-start | bytes 1507328 | tf_op jit(solution)/shard_map/all_to_all | solution.py:314
  119.0 2.3 %join.1 = bf16[2,4,4,136,360]{4,3,2,1,0:T(8,128)(2,1)S(1)} custom-call(s32[4]{0:T(128)S(1)} %get-tuple-element.53.place_ref, bf16[2,4,136,360]{3,2,1,0:T(8,128)(2,1)S(1)} %collective-permute-done.refs_0_, bf16[2,4,136,360]{3,2,1,0:T(8,128)(2,1)} %collective-permute-done.1.refs_1_, bf16[2,4,136,360]{3,2,1,0:T(8,128)(2,1)} %collective-permute-done.2.refs_2_, ...), custom_call_target="tpu_custom_call" | custom-call | tf_op jit(solution)/shard_map/join/pallas_call | solution.py:107
  121.3 1.7 copy-done.3
  123.0 8.5 %all-to-all-done.2.slots_ref = bf16[32,4,2880]{2,1,0:T(4,128)(2,1)S(1)} async-done(((bf16[32,4,2880]{2,1,0:T(4,128)(2,1)}), bf16[32,4,2880]{2,1,0:T(4,128)(2,1)S(1)}, u32[]{:S(2)}, u32[]{:S(2)}) %all-to-all-start.2) | async-done | bytes 737312 | tf_op jit(solution)/shard_map/all_to_all | solution.py:314
  131.5 48.0 %all_to_all.25.weights_ref = bf16[32,136,360]{2,1,0:T(8,128)(2,1)S(1)} all-to-all(bf16[32,136,360]{2,1,0:T(8,128)(2,1)} %bitcast.53), channel_id=1, replica_groups=mesh['zh'=4,'core'=2,'x'=4,'zl'=2,'y'=4] {'core','x','y'}, dimensions={0} | all-to-all | bytes 6266880 | tf_op jit(solution)/shard_map/all_to_all | solution.py:318
  179.5 2.5 %expert.1 = bf16[32,4,2880]{2,1,0:T(4,128)(2,1)} custom-call(bf16[32,4,2880]{2,1,0:T(4,128)(2,1)S(1)} %all-to-all-done.2.slots_ref, bf16[32,136,360]{2,1,0:T(8,128)(2,1)S(1)} %all_to_all.25.weights_ref), custom_call_target="tpu_custom_call" | custom-call | tf_op jit(solution)/shard_map/expert/pallas_call | solution.py:203
  182.1 1.7 copy-done.1
  183.8 3.9 %all-to-all-start.4 = ((bf16[32,4,2880]{2,1,0:T(4,128)(2,1)}), bf16[32,4,2880]{2,1,0:T(4,128)(2,1)S(1)}, u32[]{:S(2)}, u32[]{:S(2)}) async-start(bf16[32,4,2880]{2,1,0:T(4,128)(2,1)} %expert.1), calls=%async_computation.4 | async-start | bytes 1507328 | tf_op jit(solution)/shard_map/all_to_all | solution.py:320
  187.7 1.9 copy-done.2
  189.6 3.6 %owner.1 = (bf16[180,2880]{1,0:T(8,128)(2,1)}, bf16[180,2880]{1,0:T(8,128)(2,1)}, bf16[180,2880]{1,0:T(8,128)(2,1)}) custom-call(bf16[32,136,360]{2,1,0:T(8,128)(2,1)S(1)} %copy-done.2), custom_call_target="tpu_custom_call" | custom-call | tf_op jit(solution)/shard_map/owner/pallas_call | solution.py:231
  193.3 7.1 %all-to-all-done.4 = bf16[32,4,2880]{2,1,0:T(4,128)(2,1)S(1)} async-done(((bf16[32,4,2880]{2,1,0:T(4,128)(2,1)}), bf16[32,4,2880]{2,1,0:T(4,128)(2,1)S(1)}, u32[]{:S(2)}, u32[]{:S(2)}) %all-to-all-start.4) | async-done | bytes 737312 | tf_op jit(solution)/shard_map/all_to_all | solution.py:320
  200.9 16.1 %all-gather = bf16[16,4,2880]{2,1,0:T(4,128)(2,1)S(1)} all-gather(bf16[2,4,2880]{2,1,0:T(4,128)(2,1)S(1)} %fusion), channel_id=2, replica_groups=mesh['zh'=4,'core'=2,'x'=4,'zl'=2,'y'=4] {'zh','core'}, dimensions={0}, use_global_device_ids=true | all-gather | bytes 414720 | tf_op jit(solution)/shard_map/all_gather | solution.py:331
  (63 shorter events, 17.3 us)
Async XLA Ops:
  0.6 68.8 %copy-start = (bf16[256,2880]{0,1:T(8,128)(2,1)S(1)}, bf16[256,2880]{0,1:T(8,128)(2,1)}, u32[]{:S(2)}) copy-start(bf16[256,2880]{0,1:T(8,128)(2,1)} %param.15) | copy-start | bytes 4423684
  0.8 1.3 copy-start.6
  2.1 1.2 copy-start.7
  3.4 1.2 copy-start.8
  4.6 18.6 %copy-start.11 = (bf16[2,4,2048]{2,1,0:T(4,128)(2,1)S(1)}, bf16[2,4,2048]{2,1,0:T(4,128)(2,1)}, u32[]{:S(2)}) copy-start(bf16[2,4,2048]{2,1,0:T(4,128)(2,1)} %param.11) | copy-start | bytes 98308
  4.6 19.8 %copy-start.9 = (s32[4]{0:T(128)S(1)}, s32[4]{0:T(128)}, u32[]{:S(2)}) copy-start(s32[4]{0:T(128)} %length_ref.1) | copy-start | bytes 52
  14.5 0.9 copy-start.10
  15.4 51.2 %collective-permute-start = (bf16[2,4,136,360]{3,2,1,0:T(8,128)(2,1)}, bf16[2,4,136,360]{3,2,1,0:T(8,128)(2,1)S(1)}, u32[]{:S(2)}, u32[]{:S(2)}) collective-permute-start(bf16[2,4,136,360]{3,2,1,0:T(8,128)(2,1)} %get-tuple-element.30), channel_id=1, source_target_pairs={{0,64},{1,65},{2,66},{3,67},{4,96},{5,97},{6,98},{7,99},{8,72},{9,... | collective-permute-start | bytes 2350088 | tf_op jit(solution)/shard_map/ppermute | solution.py:276
  21.2 45.5 %collective-permute-start.1 = (bf16[2,4,136,360]{3,2,1,0:T(8,128)(2,1)}, bf16[2,4,136,360]{3,2,1,0:T(8,128)(2,1)}, u32[]{:S(2)}, u32[]{:S(2)}) collective-permute-start(bf16[2,4,136,360]{3,2,1,0:T(8,128)(2,1)} %get-tuple-element.31), channel_id=1, source_target_pairs={{0,192},{1,193},{2,194},{3,195},{4,224},{5,225},{6,226},{7,227},{8... | collective-permute-start | bytes 2350088 | tf_op jit(solution)/shard_map/ppermute | solution.py:276
  24.4 1.6 copy-start.4
  26.0 1.6 copy-start.5
  31.8 34.9 %all-to-all-start = ((f32[8,4,8,128]{3,2,1,0:T(8,128)}), f32[8,4,8,128]{3,2,1,0:T(8,128)S(1)}, u32[]{:S(2)}, u32[]{:S(2)}) async-start(f32[8,4,8,128]{3,2,1,0:T(8,128)} %attend.1), calls=%async_computation | async-start | bytes 262144 | tf_op jit(solution)/shard_map/all_to_all | solution.py:285
  38.9 60.5 %collective-permute-start.2 = (bf16[2,4,136,360]{3,2,1,0:T(8,128)(2,1)}, bf16[2,4,136,360]{3,2,1,0:T(8,128)(2,1)}, u32[]{:S(2)}, u32[]{:S(2)}) collective-permute-start(bf16[2,4,136,360]{3,2,1,0:T(8,128)(2,1)} %copy-done.10), channel_id=1, source_target_pairs={{0,128},{1,129},{2,130},{3,131},{4,160},{5,161},{6,162},{7,163},{8... | collective-permute-start | bytes 2350088 | tf_op jit(solution)/shard_map/ppermute | solution.py:276
  44.6 56.3 %collective-permute-start.3 = (bf16[2,4,136,360]{3,2,1,0:T(8,128)(2,1)S(1)}, bf16[2,4,136,360]{3,2,1,0:T(8,128)(2,1)}, u32[]{:S(2)}, u32[]{:S(2)}) collective-permute-start(bf16[2,4,136,360]{3,2,1,0:T(8,128)(2,1)S(1)} %get-tuple-element.36), channel_id=1, source_target_pairs={{0,0},{1,1},{2,2},{3,3},{4,32},{5,33},{6,34},{7,35},{8,8},{9,9},{1... | collective-permute-start | bytes 2350088 | tf_op jit(solution)/shard_map/ppermute | solution.py:276
  69.1 21.3 %copy-start.13 = (f32[2,4,4]{2,1,0:T(4,128)S(1)}, f32[2,4,4]{2,1,0:T(4,128)}, u32[]{:S(2)}) copy-start(f32[2,4,4]{2,1,0:T(4,128)} %param.21) | copy-start | bytes 388
  69.1 21.3 %copy-start.14 = (s32[2,4,4]{2,1,0:T(4,128)S(1)}, s32[2,4,4]{2,1,0:T(4,128)}, u32[]{:S(2)}) copy-start(s32[2,4,4]{2,1,0:T(4,128)} %param.20) | copy-start | bytes 388
  69.5 40.8 %copy-start.12 = (f32[2880]{0:T(1024)S(1)}, f32[2880]{0:T(1024)}, u32[]{:S(2)}) copy-start(f32[2880]{0:T(1024)} %param.16) | copy-start | bytes 34564
  70.8 39.2 %all-to-all-start.1 = ((bf16[8,8,2880]{2,1,0:T(8,128)(2,1)}), bf16[8,8,2880]{2,1,0:T(8,128)(2,1)S(1)}, u32[]{:S(2)}, u32[]{:S(2)}) async-start(bf16[8,8,2880]{2,1,0:T(8,128)(2,1)} %broadcast_in_dim.8), calls=%async_computation.1 | async-start | bytes 753664 | tf_op jit(solution)/shard_map/all_to_all | solution.py:297
  111.9 19.6 %all-to-all-start.2 = ((bf16[32,4,2880]{2,1,0:T(4,128)(2,1)}), bf16[32,4,2880]{2,1,0:T(4,128)(2,1)S(1)}, u32[]{:S(2)}, u32[]{:S(2)}) async-start(bf16[32,4,2880]{2,1,0:T(4,128)(2,1)} %copy.40), calls=%async_computation.2 | async-start | bytes 1507328 | tf_op jit(solution)/shard_map/all_to_all | solution.py:314
  121.3 1.7 copy-start.3
  182.1 1.7 copy-start.1
  183.8 16.6 %all-to-all-start.4 = ((bf16[32,4,2880]{2,1,0:T(4,128)(2,1)}), bf16[32,4,2880]{2,1,0:T(4,128)(2,1)S(1)}, u32[]{:S(2)}, u32[]{:S(2)}) async-start(bf16[32,4,2880]{2,1,0:T(4,128)(2,1)} %expert.1), calls=%async_computation.4 | async-start | bytes 1507328 | tf_op jit(solution)/shard_map/all_to_all | solution.py:320
  187.7 1.9 copy-start.2
